TPU v7x, 256 devices: a whole 4x4x8 slice. The times are simulated.
256 devices in a mesh: cam: 4 (over y), tile: 64 (over x, z, core).
Axes of the slice: x: 4, y: 4, z: 8, core: 2. Of those that a mesh axis runs over, the one named last changes fastest.
Arguments:
- positions: float32 [3, 262144], P(None, ('cam', 'tile')), may hold values from -1 to 1
- log_scales: float32 [3, 262144], P(None, ('cam', 'tile')), may hold values from -4.5 to -2.5
- rotations: float32 [4, 262144], P(None, ('cam', 'tile')), may hold values from 0.3 to 1
- opacities: float32 [262144], P(('cam', 'tile')), may hold values from -6 to -3
- colors: float32 [48, 262144], P(None, ('cam', 'tile')), may hold values from -3 to 3
- cameras: float32 [2, 4, 6], replicated, may hold values from -0.05 to 0.05
- targets: float32 [2, 4, 64, 3, 256], P(None, 'cam', 'tile'), may hold values from 0 to 1
- tile_ids: int32 [2, 4, 64], P(None, 'cam', 'tile'), may hold values from 8320 to 24448, as said below
- tile_counts: int32 [2, 4, 64], P(None, 'cam', 'tile'), may hold values from 128 to 256, as said below
- tile_lists: int32 [2, 4, 64, 256], P(None, 'cam', 'tile'), may hold values from 0 to 2047, as said below
- fetch_ids: int32 [2, 4, 64, 4, 64, 8], P(None, 'cam', 'tile'), may hold values from 0 to 1023, as said below
Outputs:
- grad_positions: float32 [3, 262144], P(None, ('cam', 'tile'))
- grad_log_scales: float32 [3, 262144], P(None, ('cam', 'tile'))
- grad_rotations: float32 [4, 262144], P(None, ('cam', 'tile'))
- grad_opacities: float32 [262144], P(('cam', 'tile'))
- grad_colors: float32 [48, 262144], P(None, ('cam', 'tile'))
Inputs may be any that keep to these rules, and one draw needn't show every extreme that they name: Within one row fetch_ids[p, c, t, a, b, :] the entries are distinct local columns of the owner at cam a, tile b, all within the block of 1024 // 64 columns that belongs to the device's row of tiles; not every slot is named by a list. `tile_lists`: entries are slots of the rendering device, distinct within a tile, in increasing order of the third coordinate of their Gaussians' positions. `tile_counts`: each device has a tile with 256 live entries in each pass. `tile_ids`: each device renders one image tile in a pass; in each pass and camera group the devices' rows are distinct and together form a window of 64 rows.
All inputs are finite; a program needn't handle non-finite values.
Results may differ from a plain program's by a relative error of at most 0.0003.
Values sent between devices are 32-bit elements; how exact they have to be, the bound alone decides.
A program may use at most 192 MiB of HBM per device.

v0:
```python
import jax
import jax.numpy as jnp
from jax import lax
from jax.experimental import pallas as pl
from jax.experimental.pallas import tpu as pltpu
from jax.sharding import PartitionSpec as P

N_CAM, N_TILE, N_DEV = 4, 64, 256
ROWS = 3
LIST, PIX, BLK = 256, 256, 32
MESH = pl.DeviceIdType.MESH
F32, BF16 = jnp.float32, jnp.bfloat16

FOCAL = 4096.0
SH_ZERO = 0.28209479177387814
SH_ONE = 0.4886025119029199
SH_TWO = [
    1.0925484305920792,
    -1.0925484305920792,
    0.31539156525252005,
    -1.0925484305920792,
    0.5462742152960396,
]
SH_THREE = [
    -0.5900435899266435,
    2.890611442640554,
    -0.4570457994644658,
    0.3731763325901154,
    -0.4570457994644658,
    1.445305721320277,
    -0.5900435899266435,
]


def matmul3(left, right):
    return [
        [
            left[i][0] * right[0][j] + left[i][1] * right[1][j] + left[i][2] * right[2][j]
            for j in range(3)
        ]
        for i in range(3)
    ]


def view_of(cam_ref):
    lane = lax.broadcasted_iota(jnp.int32, (8, 128), 1)
    view = lane // 16
    values = []
    for k in range(6):
        value = jnp.zeros((8, 128), F32)
        for c in range(N_CAM):
            for p in range(2):
                value = jnp.where(view == c * 2 + p, cam_ref[p, c, k], value)
        values.append(value)
    cos_a, sin_a = jnp.cos(values[0]), jnp.sin(values[0])
    cos_b, sin_b = jnp.cos(values[1]), jnp.sin(values[1])
    cos_c, sin_c = jnp.cos(values[2]), jnp.sin(values[2])
    rotate = [
        [cos_c * cos_b, cos_c * sin_b * sin_a - sin_c * cos_a, cos_c * sin_b * cos_a + sin_c * sin_a],
        [sin_c * cos_b, sin_c * sin_b * sin_a + cos_c * cos_a, sin_c * sin_b * cos_a - cos_c * sin_a],
        [-sin_b, cos_b * sin_a, cos_b * cos_a],
    ]
    offset = [values[3], values[4], 6.0 + values[5]]
    anchor = [
        -(rotate[0][j] * offset[0] + rotate[1][j] * offset[1] + rotate[2][j] * offset[2])
        for j in range(3)
    ]
    return [rotate[i][j] for i in range(3) for j in range(3)] + offset + anchor


def project(raw, view):
    rotate = [view[0:3], view[3:6], view[6:9]]
    offset, anchor = view[9:12], view[12:15]
    point = raw[0:3]
    viewed = [
        rotate[i][0] * point[0] + rotate[i][1] * point[1] + rotate[i][2] * point[2] + offset[i]
        for i in range(3)
    ]
    toward = [point[j] - anchor[j] for j in range(3)]
    length = jnp.sqrt(toward[0] * toward[0] + toward[1] * toward[1] + toward[2] * toward[2])
    per_length = 1.0 / length
    ux, uy, uz = (toward[0] * per_length, toward[1] * per_length, toward[2] * per_length)
    quat_norm = jnp.sqrt(raw[6] * raw[6] + raw[7] * raw[7] + raw[8] * raw[8] + raw[9] * raw[9])
    per_norm = 1.0 / quat_norm
    qw, qx, qy, qz = (raw[6] * per_norm, raw[7] * per_norm, raw[8] * per_norm, raw[9] * per_norm)
    spin = [
        [1.0 - 2.0 * (qy * qy + qz * qz), 2.0 * (qx * qy - qw * qz), 2.0 * (qx * qz + qw * qy)],
        [2.0 * (qx * qy + qw * qz), 1.0 - 2.0 * (qx * qx + qz * qz), 2.0 * (qy * qz - qw * qx)],
        [2.0 * (qx * qz - qw * qy), 2.0 * (qy * qz + qw * qx), 1.0 - 2.0 * (qx * qx + qy * qy)],
    ]
    squares = [jnp.exp(2.0 * raw[3 + k]) for k in range(3)]
    turned = matmul3(rotate, spin)

    def covariance(a, b):
        return (
            turned[a][0] * turned[b][0] * squares[0]
            + turned[a][1] * turned[b][1] * squares[1]
            + turned[a][2] * turned[b][2] * squares[2]
        )

    c00, c01, c02 = covariance(0, 0), covariance(0, 1), covariance(0, 2)
    c11, c12, c22 = covariance(1, 1), covariance(1, 2), covariance(2, 2)
    inverse = 1.0 / viewed[2]
    j_main = FOCAL * inverse
    j_side_x = -j_main * viewed[0] * inverse
    j_side_y = -j_main * viewed[1] * inverse
    s_xx = j_main * j_main * c00 + 2.0 * j_main * j_side_x * c02 + j_side_x * j_side_x * c22 + 0.3
    s_xy = (
        j_main * j_main * c01
        + j_main * j_side_y * c02
        + j_side_x * j_main * c12
        + j_side_x * j_side_y * c22
    )
    s_yy = j_main * j_main * c11 + 2.0 * j_main * j_side_y * c12 + j_side_y * j_side_y * c22 + 0.3
    per_det = 1.0 / (s_xx * s_yy - s_xy * s_xy)
    conic_a = s_yy * per_det
    conic_b = -s_xy * per_det
    conic_c = s_xx * per_det
    screen_u = j_main * viewed[0] + 2048.0
    screen_v = j_main * viewed[1] + 1024.0
    opacity = 1.0 / (1.0 + jnp.exp(-raw[10]))
    xx, yy, zz = (ux * ux, uy * uy, uz * uz)
    basis = [
        None,
        -SH_ONE * uy,
        SH_ONE * uz,
        -SH_ONE * ux,
        SH_TWO[0] * ux * uy,
        SH_TWO[1] * uy * uz,
        SH_TWO[2] * (2.0 * zz - xx - yy),
        SH_TWO[3] * ux * uz,
        SH_TWO[4] * (xx - yy),
        SH_THREE[0] * uy * (3.0 * xx - yy),
        SH_THREE[1] * ux * uy * uz,
        SH_THREE[2] * uy * (4.0 * zz - xx - yy),
        SH_THREE[3] * uz * (2.0 * zz - 3.0 * xx - 3.0 * yy),
        SH_THREE[4] * ux * (4.0 * zz - xx - yy),
        SH_THREE[5] * uz * (xx - yy),
        SH_THREE[6] * ux * (xx - 3.0 * yy),
    ]
    channels = []
    for channel in range(3):
        total = 0.5 + SH_ZERO * raw[11 + channel]
        for k in range(1, 16):
            total = total + basis[k] * raw[11 + 3 * k + channel]
        channels.append(total)
    return [screen_u, screen_v, conic_a, conic_b, conic_c, opacity] + channels


def split(value):
    high = value.astype(BF16)
    rest = value - high.astype(F32)
    mid = rest.astype(BF16)
    low = (rest - mid.astype(F32)).astype(BF16)
    return high, mid, low


def pick(chooser, value):
    high, mid, low = split(value)
    return (
        jnp.dot(chooser, high, preferred_element_type=F32)
        + jnp.dot(chooser, mid, preferred_element_type=F32)
    ) + jnp.dot(chooser, low, preferred_element_type=F32)


def turn(value, lanes):
    lanes = lanes % 128
    return value if lanes == 0 else pltpu.roll(value, lanes, 1)


def expand(refs, chunk):
    lane = lax.broadcasted_iota(jnp.int32, (8, 128), 1)
    row = lax.broadcasted_iota(jnp.int32, (8, 128), 0)
    own = lane // 16 == row
    here = pl.ds(pl.multiple_of(chunk * 128, 128), 128)
    out = []
    for ref in refs:
        for k in range(ref.shape[0]):
            value = jnp.where(own, jnp.broadcast_to(ref[k : k + 1, here], (8, 128)), 0.0)
            for step in (16, 32, 64):
                value = value + pltpu.roll(value, step, 1)
            out.append(value)
    return out


def project_kernel(pos, scl, rot, opa, col, cam, out, view_ref):
    for k, value in enumerate(view_of(cam)):
        view_ref[k] = value

    def step(chunk, carry):
        view = [view_ref[k] for k in range(15)]
        record = project(expand((pos, scl, rot, opa, col), chunk), view)
        group = lax.broadcasted_iota(jnp.int32, (8, 128), 1) // 32
        rows = pl.ds(pl.multiple_of(chunk * 8, 8), 8)
        for c in range(N_CAM):
            for m in range(ROWS):
                value = jnp.zeros((8, 128), F32)
                for q in range(4):
                    if 4 * m + q < 9:
                        value = jnp.where(group == q, turn(record[4 * m + q], (q - c) * 32), value)
                out[c * ROWS + m, rows, :] = value
        return carry

    lax.fori_loop(0, 8, step, 0)


def place():
    return lax.axis_index("cam"), lax.axis_index("tile")


def across(c, t, i):
    index = lax.rem(c * 4 + t // 16 + i, 16)
    return (index // 4, lax.rem(index, 4) * 16 + lax.rem(t, 16))


def along(c, t, i):
    return (c, (t // 16) * 16 + lax.rem(lax.rem(t, 16) + i, 16))


def greet(c, t):
    barrier = pltpu.get_barrier_semaphore()

    def hail(i, carry):
        pl.semaphore_signal(barrier, inc=1, device_id=along(c, t, i), device_id_type=MESH)
        pl.semaphore_signal(barrier, inc=1, device_id=across(c, t, i), device_id_type=MESH)
        return carry

    lax.fori_loop(1, 16, hail, 0)
    pl.semaphore_wait(barrier, 30)


def exchange(src, dst, c, t, send, recv, own):
    me = c * N_TILE + t
    local = pltpu.make_async_copy(src.at[me], dst.at[me], own)
    local.start()

    def one(i, carry):
        to = lax.rem(me + i, N_DEV)
        pltpu.make_async_remote_copy(
            src_ref=src.at[to],
            dst_ref=dst.at[me],
            send_sem=send,
            recv_sem=recv,
            device_id=(to // N_TILE, lax.rem(to, N_TILE)),
            device_id_type=MESH,
        ).start()
        return carry

    lax.fori_loop(1, N_DEV, one, 0, unroll=5)
    most = pl.ds(0, N_DEV - 1)
    pltpu.make_async_copy(src.at[most], src.at[most], send).wait()
    pltpu.make_async_copy(dst.at[most], dst.at[most], recv).wait()
    local.wait()


def forward_kernel(mine, records, table, out, packed, send_a, recv_a, own_a, send_b, recv_b, send_c, recv_c, own_c):
    c, t = place()
    me = c * N_TILE + t
    greet(c, t)
    local = pltpu.make_async_copy(mine.at[0], table.at[me], own_a)
    local.start()

    def first(i, carry):
        pltpu.make_async_remote_copy(
            src_ref=mine.at[0],
            dst_ref=table.at[me],
            send_sem=send_a,
            recv_sem=recv_a,
            device_id=along(c, t, i),
            device_id_type=MESH,
        ).start()
        return carry

    lax.fori_loop(1, 16, first, 0)
    local.wait()
    some = pl.ds(0, 15)
    pltpu.make_async_copy(table.at[some], table.at[some], send_a).wait()
    pltpu.make_async_copy(table.at[some], table.at[some], recv_a).wait()
    line = pl.ds(c * N_TILE + (t // 16) * 16, 16)

    def second(i, carry):
        pltpu.make_async_remote_copy(
            src_ref=table.at[line],
            dst_ref=table.at[line],
            send_sem=send_b,
            recv_sem=recv_b,
            device_id=across(c, t, i),
            device_id_type=MESH,
        ).start()
        return carry

    lax.fori_loop(1, 16, second, 0)
    most = pl.ds(0, 240)
    pltpu.make_async_copy(table.at[most], table.at[most], send_b).wait()
    pltpu.make_async_copy(table.at[most], table.at[most], recv_b).wait()

    lane = lax.broadcasted_iota(jnp.int32, (64, 128), 1)
    even = lax.rem(lane // 16, 2) == 0
    for g in range(N_CAM):
        wanted = table[g * N_TILE : (g + 1) * N_TILE, 0, :]
        chooser = jnp.where(wanted == lax.rem(lane, 64), 1.0, 0.0).astype(BF16)
        for m in range(ROWS):
            value = records[g * ROWS + m]
            both = jnp.concatenate([jnp.where(even, value, 0.0), jnp.where(even, 0.0, value)], axis=0)
            packed[g * N_TILE : (g + 1) * N_TILE, m, :] = pick(chooser, both)
    exchange(packed, out, c, t, send_c, recv_c, own_c)


def backward_kernel(grads, out, ready, send, recv, own):
    c, t = place()
    greet(c, t)

    def hail(i, carry):
        pl.semaphore_signal(ready, inc=1, device_id=across(c, t, i), device_id_type=MESH)
        return carry

    lax.fori_loop(1, 16, hail, 0)
    pl.semaphore_wait(ready, 15)
    exchange(grads, out, c, t, send, recv, own)


def render_kernel(place_ref, count_ref, data, fetch, list_col, list_row, target, out, cols, alpha_ref, through_ref, lost):
    lane = lax.broadcasted_iota(jnp.int32, (LIST, 128), 1)
    lane_b = lax.broadcasted_iota(jnp.int32, (BLK, 128), 1)
    row_b = lax.broadcasted_iota(jnp.int32, (BLK, 128), 0)
    lane_1 = lax.broadcasted_iota(jnp.int32, (1, 128), 1)
    parts = split(jnp.concatenate([data[:, m, :] for m in range(ROWS)], axis=1))
    blocks = LIST // BLK
    total = None
    for p in range(2):
        slot = list_col[p]
        owner = slot // 8
        spot = lax.rem(slot, 8)
        wide = lax.broadcasted_iota(jnp.int32, (LIST, N_DEV), 1)
        chooser = jnp.where(wide == owner, 1.0, 0.0).astype(BF16)
        within = lax.rem(fetch[p], 16).astype(F32).astype(BF16)
        near = jnp.dot(chooser, within, preferred_element_type=F32)
        eight = lax.broadcasted_iota(jnp.int32, near.shape, 1)
        column = jnp.sum(jnp.where(eight == spot, near, 0.0), axis=1, keepdims=True)
        live_lane = (lax.rem(lane // 16, 2) == p) & (lax.rem(lane, 16).astype(F32) == column)
        picked = jnp.dot(chooser, parts[0], preferred_element_type=F32)
        picked = picked + jnp.dot(chooser, parts[1], preferred_element_type=F32)
        picked = picked + jnp.dot(chooser, parts[2], preferred_element_type=F32)
        for v in range(9):
            m, q = v // 4, v % 4
            value = jnp.where(live_lane & (lane // 32 == q), picked[:, m * 128 : (m + 1) * 128], 0.0)
            cols[v] = jnp.broadcast_to(jnp.sum(value, axis=1, keepdims=True), (LIST, 128))
        cols[9] = jnp.where(live_lane, 1.0, 0.0)

        tile = place_ref[p]
        count = count_ref[p]
        left = (lax.rem(tile, 256) * 16).astype(F32) + 0.5
        top = ((tile // 256) * 16).astype(F32) + 0.5
        px = left + lax.rem(lane_1, 16).astype(F32)
        py = [top + ((lane_1 + h * 128) // 16).astype(F32) for h in range(2)]

        def ahead(b, carry):
            rows = pl.ds(pl.multiple_of(b * BLK, BLK), BLK)
            u, v, ca, cb, cc, o = [cols[k, rows, :] for k in range(6)]
            shade = [cols[k, rows, :] for k in (6, 7, 8)]
            live = row_b + b * BLK < count
            dx = px - u
            dxx = ca * dx * dx
            result = []
            for h in range(2):
                passed, shown = carry[h][0], carry[h][1:]
                dy = py[h] - v
                quad = dxx + 2.0 * cb * dx * dy + cc * dy * dy
                alpha = jnp.where(live, o * jnp.exp(-0.5 * quad), 0.0)
                run = 1.0 - alpha
                for s in (1, 2, 4, 8, 16):
                    run = run * jnp.where(row_b >= s, pltpu.roll(run, s, 0), 1.0)
                before = passed * jnp.where(row_b >= 1, pltpu.roll(run, 1, 0), 1.0)
                weight = alpha * before
                alpha_ref[h, rows, :] = alpha
                through_ref[h, rows, :] = before
                result.append(
                    (passed * run[BLK - 1 : BLK, :],)
                    + tuple(s + jnp.sum(k * weight, axis=0, keepdims=True) for s, k in zip(shown, shade))
                )
            return tuple(result)

        one, zero = jnp.ones((1, 128), F32), jnp.zeros((1, 128), F32)
        shown = lax.fori_loop(0, blocks, ahead, ((one, zero, zero, zero),) * 2)
        miss = [
            [shown[h][1 + k] - target[p, k : k + 1, h * 128 : (h + 1) * 128] for k in range(3)]
            for h in range(2)
        ]

        def back(i, carry):
            b = blocks - 1 - i
            rows = pl.ds(pl.multiple_of(b * BLK, BLK), BLK)
            u, v, ca, cb, cc, o = [cols[k, rows, :] for k in range(6)]
            shade = [cols[k, rows, :] for k in (6, 7, 8)]
            dx = px - u
            sums = [0.0] * 9
            result = []
            for h in range(2):
                alpha, before = alpha_ref[h, rows, :], through_ref[h, rows, :]
                dy = py[h] - v
                weight = alpha * before
                pull = shade[0] * miss[h][0] + shade[1] * miss[h][1] + shade[2] * miss[h][2]
                run = pull * weight
                for s in (1, 2, 4, 8, 16):
                    run = run + jnp.where(row_b < BLK - s, pltpu.roll(run, BLK - s, 0), 0.0)
                after = carry[h] + jnp.where(row_b < BLK - 1, pltpu.roll(run, BLK - 1, 0), 0.0)
                result.append(carry[h] + run[0:1, :])
                slope = (before * pull - after / (1.0 - alpha)) * alpha
                tilt_x, tilt_y = slope * dx, slope * dy
                terms = [tilt_x, tilt_y, tilt_x * dx, tilt_x * dy, tilt_y * dy, slope]
                terms = terms + [weight * miss[h][k] for k in range(3)]
                sums = [a + t for a, t in zip(sums, terms)]
            m_x, m_y, m_xx, m_xy, m_yy, m_0, *g_shade = [jnp.sum(s, axis=1, keepdims=True) for s in sums]
            grads = [
                ca * m_x + cb * m_y,
                cb * m_x + cc * m_y,
                -0.5 * m_xx,
                -m_xy,
                -0.5 * m_yy,
                m_0 / o,
            ] + g_shade
            keep = cols[9, rows, :]
            for m in range(ROWS):
                value = jnp.zeros((BLK, 128), F32)
                for q in range(4):
                    if 4 * m + q < 9:
                        value = jnp.where(lane_b // 32 == q, jnp.broadcast_to(grads[4 * m + q], (BLK, 128)), value)
                lost[rows, m * 128 : (m + 1) * 128] = value * keep
            return tuple(result)

        lax.fori_loop(0, blocks, back, (zero, zero))
        tall = lax.broadcasted_iota(jnp.int32, (N_DEV, LIST), 0)
        giver = jnp.where(tall == list_row[p] // 8, 1.0, 0.0).astype(BF16)
        part = pick(giver, lost[...])
        total = part if total is None else total + part
    for m in range(ROWS):
        out[:, m, :] = total[:, m * 128 : (m + 1) * 128]


def gradient_kernel(pos, scl, rot, opa, col, cam, table, arrived, g_pos, g_scl, g_rot, g_opa, g_col, view_ref, cot):
    for k, value in enumerate(view_of(cam)):
        view_ref[k] = value
    lane = lax.broadcasted_iota(jnp.int32, (64, 128), 1)
    even = lax.rem(lane // 16, 2) == 0
    for g in range(N_CAM):
        wanted = table[g * N_TILE : (g + 1) * N_TILE, 0, :]
        chooser = jnp.where(wanted == lax.rem(lane, 64), 1.0, 0.0).T.astype(BF16)
        for m in range(ROWS):
            both = pick(chooser, arrived[g * N_TILE : (g + 1) * N_TILE, m, :])
            value = jnp.where(even, both[0:64], both[64:128])
            for q in range(4):
                v = 4 * m + q
                if v < 9:
                    turned = turn(value, (g - q) * 32)
                    if g == 0:
                        cot[v] = turned
                    else:
                        cot[v] = jnp.where(lane // 32 == g, turned, cot[v])
    own_lane = lax.broadcasted_iota(jnp.int32, (8, 128), 1) // 16
    own = own_lane == lax.broadcasted_iota(jnp.int32, (8, 128), 0)

    def step(chunk, carry):
        view = [view_ref[k] for k in range(15)]
        raw = expand((pos, scl, rot, opa, col), chunk)
        rows = pl.ds(pl.multiple_of(chunk * 8, 8), 8)
        here = pl.ds(pl.multiple_of(chunk * 128, 128), 128)
        _, pull = jax.vjp(lambda values: project(values, view), raw)
        (grads,) = pull([cot[v, rows, :] for v in range(9)])
        k = 0
        for ref in (g_pos, g_scl, g_rot, g_opa, g_col):
            for r in range(ref.shape[0]):
                value = grads[k]
                for s in (16, 32, 64):
                    value = value + pltpu.roll(value, s, 1)
                ref[r : r + 1, here] = jnp.sum(jnp.where(own, value, 0.0), axis=0, keepdims=True)
                k += 1
        return carry

    lax.fori_loop(0, 8, step, 0)


VMEM = pl.BlockSpec(memory_space=pltpu.VMEM)
SMEM = pl.BlockSpec(memory_space=pltpu.SMEM)
DMA = pltpu.SemaphoreType.DMA


def shape(*dims, dtype=F32):
    return jax.ShapeDtypeStruct(dims, dtype)


def body(
    positions,
    log_scales,
    rotations,
    opacities,
    colors,
    cameras,
    targets,
    tile_ids,
    tile_counts,
    tile_lists,
    fetch_ids,
):
    params = (positions, log_scales, rotations, opacities.reshape(1, 1024), colors)
    records = pl.pallas_call(
        project_kernel,
        out_shape=shape(12, 64, 128),
        in_specs=[VMEM] * 5 + [SMEM],
        out_specs=VMEM,
        scratch_shapes=[pltpu.VMEM((15, 8, 128), F32)],
    )(*params, cameras)

    fetched = fetch_ids.reshape(2, N_DEV, 8)
    block = fetched[:, 0, 0] // 16
    mine = jnp.repeat(block, 64).reshape(1, 1, 128)
    table, data = pl.pallas_call(
        forward_kernel,
        out_shape=(shape(N_DEV, 1, 128, dtype=jnp.int32), shape(N_DEV, ROWS, 128)),
        in_specs=[VMEM] * 2,
        out_specs=(VMEM, VMEM),
        scratch_shapes=[pltpu.VMEM((N_DEV, ROWS, 128), F32)] + [DMA] * 8,
        compiler_params=pltpu.CompilerParams(collective_id=0, has_side_effects=True),
    )(mine, records)

    lists = tile_lists.reshape(2, LIST)
    record_grads = pl.pallas_call(
        render_kernel,
        out_shape=shape(N_DEV, ROWS, 128),
        in_specs=[SMEM] * 2 + [VMEM] * 5,
        out_specs=VMEM,
        scratch_shapes=[
            pltpu.VMEM((10, LIST, 128), F32),
            pltpu.VMEM((2, LIST, 128), F32),
            pltpu.VMEM((2, LIST, 128), F32),
            pltpu.VMEM((LIST, 3 * 128), F32),
        ],
    )(
        tile_ids.reshape(2),
        tile_counts.reshape(2),
        data,
        fetched,
        lists.reshape(2, LIST, 1),
        lists.reshape(2, 1, LIST),
        targets.reshape(2, 3, PIX),
    )

    returned = pl.pallas_call(
        backward_kernel,
        out_shape=shape(N_DEV, ROWS, 128),
        in_specs=[VMEM],
        out_specs=VMEM,
        scratch_shapes=[pltpu.SemaphoreType.REGULAR] + [DMA] * 3,
        compiler_params=pltpu.CompilerParams(collective_id=1, has_side_effects=True),
    )(record_grads)

    g_pos, g_scl, g_rot, g_opa, g_col = pl.pallas_call(
        gradient_kernel,
        out_shape=tuple(shape(n, 1024) for n in (3, 3, 4, 1, 48)),
        in_specs=[VMEM] * 5 + [SMEM] + [VMEM] * 2,
        out_specs=(VMEM,) * 5,
        scratch_shapes=[pltpu.VMEM((15, 8, 128), F32), pltpu.VMEM((9, 64, 128), F32)],
    )(*params, cameras, table, returned)
    return g_pos, g_scl, g_rot, g_opa.reshape(1024), g_col


def solution(mesh):
    return jax.shard_map(
        body,
        mesh=mesh,
        in_specs=(
            P(None, ("cam", "tile")),
            P(None, ("cam", "tile")),
            P(None, ("cam", "tile")),
            P(("cam", "tile")),
            P(None, ("cam", "tile")),
            P(),
            P(None, "cam", "tile", None, None),
            P(None, "cam", "tile"),
            P(None, "cam", "tile"),
            P(None, "cam", "tile", None),
            P(None, "cam", "tile", None, None, None),
        ),
        out_specs=(
            P(None, ("cam", "tile")),
            P(None, ("cam", "tile")),
            P(None, ("cam", "tile")),
            P(("cam", "tile")),
            P(None, ("cam", "tile")),
        ),
        check_vma=False,
    )
```

profile of v0, /device:TPU:1, one launch (start us, length us, event | category | flops | bytes accessed | tf_op | source)
XLA Modules:
  0.0 84.5 jit_solution(16986747584501470261)
XLA Ops:
  0.6 0.9 %copy.17 = s32[2,1,1,4,64,8]{5,4,3,0,2,1:T(8,128)S(1)} copy(s32[2,1,1,4,64,8]{4,5,3,2,1,0:T(8,128)} %param.21) | data formatting | bytes 32768 | tf_op args[10]
  1.5 0.0 copy-start
  1.5 0.1 slice_reduce_fusion
  1.7 0.1 broadcast_in_dim.3
  1.7 0.6 reshape_reshape.9.mine
  2.3 5.1 %shard_map.146.records = f32[12,64,128]{2,1,0:T(8,128)} custom-call(f32[3,1024]{1,0:T(4,128)} %pos.3, f32[3,1024]{1,0:T(4,128)} %scl.3, f32[4,1024]{1,0:T(4,128)} %rot.3, f32[1,1024]{1,0:T(1,128)} %bitcast.12, f32[48,1024]{1,0:T(8,128)} %col.3, f32[2,4,6]{2,1,0:T(4,128)} %cam.3), custom_call_target="tpu_custom_call" | custom-call | tf_op jit(solution)/shard_map/pallas_call | solution.py:505
  7.5 0.0 copy-done
  7.5 34.0 %shard_map.147 = (s32[256,1,128]{2,1,0:T(1,128)}, f32[256,3,128]{2,1,0:T(4,128)}) custom-call(s32[1,1,128]{2,1,0:T(1,128)} %reshape_reshape.9.mine, f32[12,64,128]{2,1,0:T(8,128)} %shard_map.146.records), custom_call_target="tpu_custom_call" | custom-call | tf_op jit(solution)/shard_map/pallas_call | solution.py:516
  41.5 0.0 copy-start.1
  41.5 0.7 copy-done.1
  42.2 0.0 copy-start.2
  42.2 0.9 %reshape_reshape.12.list_col = s32[2,256,1]{2,1,0:T(8,128)} reshape(s32[2,256]{1,0:T(2,128)S(1)} %reduce.1) | data formatting | bytes 4096 | tf_op jit(solution)/shard_map/reshape;reshape | solution.py:542
  43.0 0.0 copy-done.2
  43.0 0.6 copy.20.target
  43.6 7.8 %shard_map.148.grads = f32[256,3,128]{2,1,0:T(4,128)} custom-call(s32[2]{0:T(128)} %bitcast.15, s32[2]{0:T(128)} %bitcast.16, f32[256,3,128]{2,1,0:T(4,128)} %get-tuple-element.13.data, s32[2,256,8]{2,1,0:T(8,128)} %bitcast.10, s32[2,256,1]{2,1,0:T(8,128)} %reshape_reshape.12.list_col, s32[2,1,256]{2,1,0:T(1,128)} %bitcast.14, f32[2,3,256]{2,1,0:T(4,128)} %copy.20.target), custom_call_target="tpu_custom_call" | custom-call | tf_op jit(solution)/shard_map/pallas_call | solution.py:526
  51.4 20.8 %shard_map.149.arrived = f32[256,3,128]{2,1,0:T(4,128)} custom-call(f32[256,3,128]{2,1,0:T(4,128)} %shard_map.148.grads), custom_call_target="tpu_custom_call" | custom-call | tf_op jit(solution)/shard_map/pallas_call | solution.py:547
  72.2 12.3 %shard_map.150 = (f32[3,1024]{1,0:T(4,128)}, f32[3,1024]{1,0:T(4,128)}, f32[4,1024]{1,0:T(4,128)}, f32[1,1024]{1,0:T(1,128)}, f32[48,1024]{1,0:T(8,128)}) custom-call(f32[3,1024]{1,0:T(4,128)} %pos.3, f32[3,1024]{1,0:T(4,128)} %scl.3, f32[4,1024]{1,0:T(4,128)} %rot.3, f32[1,1024]{1,0:T(1,128)} %bitcast.13, f32[48,1024]{1,0:T(8,128)} %col.3, f32[2,4,6]{2,1,0:T(4,128)} %cam.3, ...), custom_call_target="tpu_custom_call" | custom-call | tf_op jit(solution)/shard_map/pallas_call | solution.py:556
  (3 shorter events, 0.0 us)
Async XLA Ops:
  1.5 6.0 %copy-start = (s32[2,1,1,4,64,8]{5,4,3,0,2,1:T(8,128)}, s32[2,1,1,4,64,8]{5,4,3,0,2,1:T(8,128)S(1)}, u32[]{:S(2)}) copy-start(s32[2,1,1,4,64,8]{5,4,3,0,2,1:T(8,128)S(1)} %copy.17) | copy-start | bytes 49156
  41.5 0.7 copy-start.1
  42.2 0.9 %copy-start.2 = (f32[2,1,1,3,256]{4,2,3,1,0:T(1,128)S(1)}, f32[2,1,1,3,256]{4,2,3,1,0:T(1,128)}, u32[]{:S(2)}) copy-start(f32[2,1,1,3,256]{4,2,3,1,0:T(1,128)} %param.17) | copy-start | bytes 18436
where the time goes:
time: 84.8 us; the launch traced here: 84.5 us
  Pallas kernels  80 us (94%)
  local copies, waits for them, and re-layouts  3.81 us (4%)
    pallas_call x1, Pallas kernels, body(): pl.pallas_call(forward_kernel, out_shape=(shape(N_DEV, 1, 128, dtype=jnp....  34 us
    pallas_call x1, Pallas kernels, body(): pl.pallas_call(backward_kernel, out_shape=shape(N_DEV, ROWS, 128), in_spe...  20.8 us
    pallas_call x1, Pallas kernels, body(): pl.pallas_call(gradient_kernel, out_shape=tuple((shape(n, 1024) for n in...  12.3 us
    pallas_call x1, Pallas kernels, body(): pl.pallas_call(render_kernel, out_shape=shape(N_DEV, ROWS, 128), in_specs...  7.79 us
    pallas_call x1, Pallas kernels, body(): pl.pallas_call(project_kernel, out_shape=shape(12, 64, 128), in_specs=[VM...  5.15 us

commit v1 on v0

--- a/solution.py
+++ b/solution.py
@@ -168,40 +168,41 @@
     return value if lanes == 0 else pltpu.roll(value, lanes, 1)
 
 
-def expand(refs, chunk):
-    lane = lax.broadcasted_iota(jnp.int32, (8, 128), 1)
-    row = lax.broadcasted_iota(jnp.int32, (8, 128), 0)
-    own = lane // 16 == row
-    here = pl.ds(pl.multiple_of(chunk * 128, 128), 128)
-    out = []
+def spread_of(first):
+    lane = lax.broadcasted_iota(jnp.int32, (128, 256), 1)
+    row = lax.broadcasted_iota(jnp.int32, (128, 256), 0)
+    return jnp.where(row == (first + lane // 128) * 16 + lax.rem(lane, 16), 1.0, 0.0).astype(BF16)
+
+
+def expand(refs, flat, wide):
+    flat[56:64, :] = jnp.zeros((8, 1024), F32)
+    start = 0
     for ref in refs:
-        for k in range(ref.shape[0]):
-            value = jnp.where(own, jnp.broadcast_to(ref[k : k + 1, here], (8, 128)), 0.0)
-            for step in (16, 32, 64):
-                value = value + pltpu.roll(value, step, 1)
-            out.append(value)
-    return out
-
-
-def project_kernel(pos, scl, rot, opa, col, cam, out, view_ref):
-    for k, value in enumerate(view_of(cam)):
-        view_ref[k] = value
-
-    def step(chunk, carry):
-        view = [view_ref[k] for k in range(15)]
-        record = project(expand((pos, scl, rot, opa, col), chunk), view)
-        group = lax.broadcasted_iota(jnp.int32, (8, 128), 1) // 32
-        rows = pl.ds(pl.multiple_of(chunk * 8, 8), 8)
-        for c in range(N_CAM):
-            for m in range(ROWS):
-                value = jnp.zeros((8, 128), F32)
-                for q in range(4):
-                    if 4 * m + q < 9:
-                        value = jnp.where(group == q, turn(record[4 * m + q], (q - c) * 32), value)
-                out[c * ROWS + m, rows, :] = value
-        return carry
-
-    lax.fori_loop(0, 8, step, 0)
+        flat[start : start + ref.shape[0], :] = ref[...]
+        start += ref.shape[0]
+    parts = split(jnp.concatenate([flat[:, j * 128 : (j + 1) * 128] for j in range(8)], axis=0))
+    for i in range(0, 8, 2):
+        spread = spread_of(i)
+        value = (
+            jnp.dot(parts[0], spread, preferred_element_type=F32)
+            + jnp.dot(parts[1], spread, preferred_element_type=F32)
+        ) + jnp.dot(parts[2], spread, preferred_element_type=F32)
+        wide[:, i, :] = value[:, 0:128]
+        wide[:, i + 1, :] = value[:, 128:256]
+
+
+def project_chunk(chunk, wide, view_ref, out):
+    view = [view_ref[k] for k in range(15)]
+    record = project([wide[chunk * 64 + k] for k in range(59)], view)
+    group = lax.broadcasted_iota(jnp.int32, (8, 128), 1) // 32
+    rows = pl.ds(pl.multiple_of(chunk * 8, 8), 8)
+    for c in range(N_CAM):
+        for m in range(ROWS):
+            value = jnp.zeros((8, 128), F32)
+            for q in range(4):
+                if 4 * m + q < 9:
+                    value = jnp.where(group == q, turn(record[4 * m + q], (q - c) * 32), value)
+            out[c * ROWS + m, rows, :] = value
 
 
 def place():
@@ -226,13 +227,11 @@
         return carry
 
     lax.fori_loop(1, 16, hail, 0)
-    pl.semaphore_wait(barrier, 30)
-
-
-def exchange(src, dst, c, t, send, recv, own):
+    return barrier
+
+
+def send_rows(src, dst, c, t, send, recv, low, high):
     me = c * N_TILE + t
-    local = pltpu.make_async_copy(src.at[me], dst.at[me], own)
-    local.start()
 
     def one(i, carry):
         to = lax.rem(me + i, N_DEV)
@@ -246,19 +245,68 @@
         ).start()
         return carry
 
-    lax.fori_loop(1, N_DEV, one, 0, unroll=5)
+    lax.fori_loop(low, high, one, 0, unroll=5)
+
+
+def wait_rows(src, dst, send, recv):
     most = pl.ds(0, N_DEV - 1)
     pltpu.make_async_copy(src.at[most], src.at[most], send).wait()
     pltpu.make_async_copy(dst.at[most], dst.at[most], recv).wait()
-    local.wait()
-
-
-def forward_kernel(mine, records, table, out, packed, send_a, recv_a, own_a, send_b, recv_b, send_c, recv_c, own_c):
+
+
+def main_kernel(
+    place_ref,
+    count_ref,
+    cam,
+    pos,
+    scl,
+    rot,
+    opa,
+    col,
+    mine,
+    fetch,
+    list_col,
+    list_row,
+    target,
+    table,
+    returned,
+    flat,
+    wide,
+    view_ref,
+    records,
+    packed,
+    data,
+    grads,
+    cols,
+    alpha_ref,
+    through_ref,
+    lost,
+    send_a,
+    recv_a,
+    own_a,
+    send_b,
+    recv_b,
+    send_c,
+    recv_c,
+    own_c,
+    send_d,
+    recv_d,
+    own_d,
+):
     c, t = place()
     me = c * N_TILE + t
-    greet(c, t)
+    barrier = greet(c, t)
     local = pltpu.make_async_copy(mine.at[0], table.at[me], own_a)
     local.start()
+    for k, value in enumerate(view_of(cam)):
+        view_ref[k] = value
+    expand((pos, scl, rot, opa, col), flat, wide)
+
+    def step(chunk, carry):
+        project_chunk(chunk, wide, view_ref, records)
+        return carry
+
+    pl.semaphore_wait(barrier, 30)
 
     def first(i, carry):
         pltpu.make_async_remote_copy(
@@ -272,6 +320,7 @@
         return carry
 
     lax.fori_loop(1, 16, first, 0)
+    lax.fori_loop(0, 4, step, 0)
     local.wait()
     some = pl.ds(0, 15)
     pltpu.make_async_copy(table.at[some], table.at[some], send_a).wait()
@@ -290,6 +339,7 @@
         return carry
 
     lax.fori_loop(1, 16, second, 0)
+    lax.fori_loop(4, 8, step, 0)
     most = pl.ds(0, 240)
     pltpu.make_async_copy(table.at[most], table.at[most], send_b).wait()
     pltpu.make_async_copy(table.at[most], table.at[most], recv_b).wait()
@@ -303,23 +353,20 @@
             value = records[g * ROWS + m]
             both = jnp.concatenate([jnp.where(even, value, 0.0), jnp.where(even, 0.0, value)], axis=0)
             packed[g * N_TILE : (g + 1) * N_TILE, m, :] = pick(chooser, both)
-    exchange(packed, out, c, t, send_c, recv_c, own_c)
-
-
-def backward_kernel(grads, out, ready, send, recv, own):
-    c, t = place()
-    greet(c, t)
-
-    def hail(i, carry):
-        pl.semaphore_signal(ready, inc=1, device_id=across(c, t, i), device_id_type=MESH)
-        return carry
-
-    lax.fori_loop(1, 16, hail, 0)
-    pl.semaphore_wait(ready, 15)
-    exchange(grads, out, c, t, send, recv, own)
-
-
-def render_kernel(place_ref, count_ref, data, fetch, list_col, list_row, target, out, cols, alpha_ref, through_ref, lost):
+    local = pltpu.make_async_copy(packed.at[me], data.at[me], own_c)
+    local.start()
+    send_rows(packed, data, c, t, send_c, recv_c, 1, N_DEV)
+    local.wait()
+    wait_rows(packed, data, send_c, recv_c)
+    render(place_ref, count_ref, data, fetch, list_col, list_row, target, grads, cols, alpha_ref, through_ref, lost)
+    local = pltpu.make_async_copy(grads.at[me], returned.at[me], own_d)
+    local.start()
+    send_rows(grads, returned, c, t, send_d, recv_d, 1, N_DEV)
+    local.wait()
+    wait_rows(grads, returned, send_d, recv_d)
+
+
+def render(place_ref, count_ref, data, fetch, list_col, list_row, target, out, cols, alpha_ref, through_ref, lost):
     lane = lax.broadcasted_iota(jnp.int32, (LIST, 128), 1)
     lane_b = lax.broadcasted_iota(jnp.int32, (BLK, 128), 1)
     row_b = lax.broadcasted_iota(jnp.int32, (BLK, 128), 0)
@@ -437,9 +484,12 @@
         out[:, m, :] = total[:, m * 128 : (m + 1) * 128]
 
 
-def gradient_kernel(pos, scl, rot, opa, col, cam, table, arrived, g_pos, g_scl, g_rot, g_opa, g_col, view_ref, cot):
+def gradient_kernel(
+    cam, pos, scl, rot, opa, col, table, arrived, g_pos, g_scl, g_rot, g_opa, g_col, flat, wide, slope, view_ref, cot
+):
     for k, value in enumerate(view_of(cam)):
         view_ref[k] = value
+    expand((pos, scl, rot, opa, col), flat, wide)
     lane = lax.broadcasted_iota(jnp.int32, (64, 128), 1)
     even = lax.rem(lane // 16, 2) == 0
     for g in range(N_CAM):
@@ -456,27 +506,35 @@
                         cot[v] = turned
                     else:
                         cot[v] = jnp.where(lane // 32 == g, turned, cot[v])
-    own_lane = lax.broadcasted_iota(jnp.int32, (8, 128), 1) // 16
-    own = own_lane == lax.broadcasted_iota(jnp.int32, (8, 128), 0)
 
     def step(chunk, carry):
         view = [view_ref[k] for k in range(15)]
-        raw = expand((pos, scl, rot, opa, col), chunk)
+        raw = [wide[chunk * 64 + k] for k in range(59)]
         rows = pl.ds(pl.multiple_of(chunk * 8, 8), 8)
-        here = pl.ds(pl.multiple_of(chunk * 128, 128), 128)
         _, pull = jax.vjp(lambda values: project(values, view), raw)
         (grads,) = pull([cot[v, rows, :] for v in range(9)])
-        k = 0
+        for k in range(59):
+            slope[chunk * 64 + k] = grads[k]
+        for k in range(59, 64):
+            slope[chunk * 64 + k] = jnp.zeros((8, 128), F32)
+        return carry
+
+    lax.fori_loop(0, 8, step, 0)
+    total = jnp.zeros((512, 128), F32)
+    into = lax.broadcasted_iota(jnp.int32, (256, 128), 1)
+    taken = lax.broadcasted_iota(jnp.int32, (256, 128), 0)
+    for i in range(0, 8, 2):
+        gather = jnp.where((into // 16 == i + taken // 128) & (lax.rem(into, 16) == lax.rem(taken, 16)), 1.0, 0.0).astype(BF16)
+        high, mid, low = split(jnp.concatenate([slope[:, i, :], slope[:, i + 1, :]], axis=1))
+        total = total + (
+            (jnp.dot(high, gather, preferred_element_type=F32) + jnp.dot(mid, gather, preferred_element_type=F32))
+            + jnp.dot(low, gather, preferred_element_type=F32)
+        )
+    for j in range(8):
+        start = j * 64
         for ref in (g_pos, g_scl, g_rot, g_opa, g_col):
-            for r in range(ref.shape[0]):
-                value = grads[k]
-                for s in (16, 32, 64):
-                    value = value + pltpu.roll(value, s, 1)
-                ref[r : r + 1, here] = jnp.sum(jnp.where(own, value, 0.0), axis=0, keepdims=True)
-                k += 1
-        return carry
-
-    lax.fori_loop(0, 8, step, 0)
+            ref[:, j * 128 : (j + 1) * 128] = total[start : start + ref.shape[0], :]
+            start += ref.shape[0]
 
 
 VMEM = pl.BlockSpec(memory_space=pltpu.VMEM)
@@ -502,64 +560,57 @@
     fetch_ids,
 ):
     params = (positions, log_scales, rotations, opacities.reshape(1, 1024), colors)
-    records = pl.pallas_call(
-        project_kernel,
-        out_shape=shape(12, 64, 128),
-        in_specs=[VMEM] * 5 + [SMEM],
-        out_specs=VMEM,
-        scratch_shapes=[pltpu.VMEM((15, 8, 128), F32)],
-    )(*params, cameras)
-
     fetched = fetch_ids.reshape(2, N_DEV, 8)
     block = fetched[:, 0, 0] // 16
     mine = jnp.repeat(block, 64).reshape(1, 1, 128)
-    table, data = pl.pallas_call(
-        forward_kernel,
+    lists = tile_lists.reshape(2, LIST)
+    spread_scratch = [
+        pltpu.VMEM((64, 1024), F32),
+        pltpu.VMEM((512, 8, 128), F32),
+    ]
+    table, returned = pl.pallas_call(
+        main_kernel,
         out_shape=(shape(N_DEV, 1, 128, dtype=jnp.int32), shape(N_DEV, ROWS, 128)),
-        in_specs=[VMEM] * 2,
+        in_specs=[SMEM] * 3 + [VMEM] * 10,
         out_specs=(VMEM, VMEM),
-        scratch_shapes=[pltpu.VMEM((N_DEV, ROWS, 128), F32)] + [DMA] * 8,
-        compiler_params=pltpu.CompilerParams(collective_id=0, has_side_effects=True),
-    )(mine, records)
-
-    lists = tile_lists.reshape(2, LIST)
-    record_grads = pl.pallas_call(
-        render_kernel,
-        out_shape=shape(N_DEV, ROWS, 128),
-        in_specs=[SMEM] * 2 + [VMEM] * 5,
-        out_specs=VMEM,
-        scratch_shapes=[
+        scratch_shapes=spread_scratch
+        + [
+            pltpu.VMEM((15, 8, 128), F32),
+            pltpu.VMEM((12, 64, 128), F32),
+            pltpu.VMEM((N_DEV, ROWS, 128), F32),
+            pltpu.VMEM((N_DEV, ROWS, 128), F32),
+            pltpu.VMEM((N_DEV, ROWS, 128), F32),
             pltpu.VMEM((10, LIST, 128), F32),
             pltpu.VMEM((2, LIST, 128), F32),
             pltpu.VMEM((2, LIST, 128), F32),
             pltpu.VMEM((LIST, 3 * 128), F32),
-        ],
+        ]
+        + [DMA] * 11,
+        compiler_params=pltpu.CompilerParams(collective_id=0, has_side_effects=True),
     )(
         tile_ids.reshape(2),
         tile_counts.reshape(2),
-        data,
+        cameras,
+        *params,
+        mine,
         fetched,
         lists.reshape(2, LIST, 1),
         lists.reshape(2, 1, LIST),
         targets.reshape(2, 3, PIX),
     )
 
-    returned = pl.pallas_call(
-        backward_kernel,
-        out_shape=shape(N_DEV, ROWS, 128),
-        in_specs=[VMEM],
-        out_specs=VMEM,
-        scratch_shapes=[pltpu.SemaphoreType.REGULAR] + [DMA] * 3,
-        compiler_params=pltpu.CompilerParams(collective_id=1, has_side_effects=True),
-    )(record_grads)
-
     g_pos, g_scl, g_rot, g_opa, g_col = pl.pallas_call(
         gradient_kernel,
         out_shape=tuple(shape(n, 1024) for n in (3, 3, 4, 1, 48)),
-        in_specs=[VMEM] * 5 + [SMEM] + [VMEM] * 2,
+        in_specs=[SMEM] + [VMEM] * 7,
         out_specs=(VMEM,) * 5,
-        scratch_shapes=[pltpu.VMEM((15, 8, 128), F32), pltpu.VMEM((9, 64, 128), F32)],
-    )(*params, cameras, table, returned)
+        scratch_shapes=spread_scratch
+        + [
+            pltpu.VMEM((512, 8, 128), F32),
+            pltpu.VMEM((15, 8, 128), F32),
+            pltpu.VMEM((9, 64, 128), F32),
+        ],
+    )(cameras, *params, table, returned)
     return g_pos, g_scl, g_rot, g_opa.reshape(1024), g_col
 
 

time: 84.8 us -> 67 us (0.79)
  Pallas kernels: 80 us -> 63 us
    pallas_call x4 -> x1, Pallas kernels: 67.7 us -> 53.5 us  [body(): pl.pallas_call(main_kernel, out_shape=(shape(N_DEV, 1, 128, dtype=jnp.int...]
    pallas_call x1, Pallas kernels: 12.3 us -> 9.57 us  [body(): pl.pallas_call(gradient_kernel, out_shape=tuple((shape(n, 1024) for n in...]
where the time goes in v1:
time: 67 us; the launch traced here: 66.8 us
  Pallas kernels  63 us (94%)
  local copies, waits for them, and re-layouts  3.04 us (5%)
  between operations  0.69 us (1%)
    pallas_call x1, Pallas kernels, body(): pl.pallas_call(main_kernel, out_shape=(shape(N_DEV, 1, 128, dtype=jnp.int...  53.5 us
    pallas_call x1, Pallas kernels, body(): pl.pallas_call(gradient_kernel, out_shape=tuple((shape(n, 1024) for n in...  9.57 us

profile of v1, /device:TPU:1, one launch (start us, length us, event | category | flops | bytes accessed | tf_op | source)
XLA Modules:
  0.0 66.8 jit_solution(11273524236627546844)
XLA Ops:
  0.6 0.0 copy-start.2
  0.6 0.0 copy-start.3
  0.7 0.7 copy-done.2
  1.3 0.0 copy-done.3
  1.4 0.6 copy.20.target
  2.0 0.0 copy-start.1
  2.0 0.8 %reshape_reshape.12.list_col = s32[2,256,1]{2,1,0:T(8,128)} reshape(s32[2,256]{1,0:T(2,128)S(1)} %reduce.1) | data formatting | bytes 4096 | tf_op jit(solution)/shard_map/reshape;reshape | solution.py:597
  2.8 0.0 copy-done.1
  2.8 0.1 copy.17
  2.9 0.0 copy-start
  2.9 0.1 slice_reduce_fusion
  3.1 0.1 broadcast_in_dim.3
  3.1 0.6 reshape_reshape.9.mine
  3.7 0.0 copy-done
  3.8 53.5 %shard_map.146 = (s32[256,1,128]{2,1,0:T(1,128)}, f32[256,3,128]{2,1,0:T(4,128)}) custom-call(s32[2]{0:T(128)} %bitcast.15, s32[2]{0:T(128)} %bitcast.16, f32[2,4,6]{2,1,0:T(4,128)} %cam.3, f32[3,1024]{1,0:T(4,128)} %pos.3, f32[3,1024]{1,0:T(4,128)} %scl.3, f32[4,1024]{1,0:T(4,128)} %rot.3, f32[1,1024]{1,0:T(1,128)} %bitcast.12, f32[48,1024]{1,0:T(8,128)} %col.3, ...), custom_call_target="tpu_custom_call" | custom-call | tf_op jit(solution)/shard_map/pallas_call | solution.py:571
  57.2 9.6 %shard_map.147 = (f32[3,1024]{1,0:T(4,128)}, f32[3,1024]{1,0:T(4,128)}, f32[4,1024]{1,0:T(4,128)}, f32[1,1024]{1,0:T(1,128)}, f32[48,1024]{1,0:T(8,128)}) custom-call(f32[2,4,6]{2,1,0:T(4,128)} %cam.3, f32[3,1024]{1,0:T(4,128)} %pos.3, f32[3,1024]{1,0:T(4,128)} %scl.3, f32[4,1024]{1,0:T(4,128)} %rot.3, f32[1,1024]{1,0:T(1,128)} %bitcast.13, f32[48,1024]{1,0:T(8,128)} %col.3, ...), custom_call_target="tpu_custom_call" | custom-call | tf_op jit(solution)/shard_map/pallas_call | solution.py:602
  (3 shorter events, 0.0 us)
Async XLA Ops:
  0.6 0.7 %copy-start.2 = (s32[2,1,1,256]{3,2,1,0:T(1,128)S(1)}, s32[2,1,1,256]{3,2,1,0:T(1,128)}, u32[]{:S(2)}) copy-start(s32[2,1,1,256]{3,2,1,0:T(1,128)} %param.20) | copy-start | bytes 6148
  0.6 0.7 %copy-start.3 = (f32[2,1,1,3,256]{4,2,3,1,0:T(1,128)S(1)}, f32[2,1,1,3,256]{4,2,3,1,0:T(1,128)}, u32[]{:S(2)}) copy-start(f32[2,1,1,3,256]{4,2,3,1,0:T(1,128)} %param.17) | copy-start | bytes 18436
  2.0 0.8 %copy-start.1 = (s32[2,1,1,4,64,8]{4,5,3,2,1,0:T(8,128)S(1)}, s32[2,1,1,4,64,8]{4,5,3,2,1,0:T(8,128)}, u32[]{:S(2)}) copy-start(s32[2,1,1,4,64,8]{4,5,3,2,1,0:T(8,128)} %param.21) | copy-start | bytes 49156
  2.9 0.8 %copy-start = (s32[2,1,1,4,64,8]{5,4,3,0,2,1:T(8,128)}, s32[2,1,1,4,64,8]{5,4,3,0,2,1:T(8,128)S(1)}, u32[]{:S(2)}) copy-start(s32[2,1,1,4,64,8]{5,4,3,0,2,1:T(8,128)S(1)} %copy.17) | copy-start | bytes 49156

commit v2 on v1

v2 whole, which is shorter than its diff:
```python
import jax
import jax.numpy as jnp
from jax import lax
from jax.experimental import pallas as pl
from jax.experimental.pallas import tpu as pltpu
from jax.sharding import PartitionSpec as P

N_CAM, N_TILE, N_DEV = 4, 64, 256
LIST, PIX, BLK = 256, 256, 32
MESH = pl.DeviceIdType.MESH
F32, BF16 = jnp.float32, jnp.bfloat16

FOCAL = 4096.0
SH_ZERO = 0.28209479177387814
SH_ONE = 0.4886025119029199
SH_TWO = [
    1.0925484305920792,
    -1.0925484305920792,
    0.31539156525252005,
    -1.0925484305920792,
    0.5462742152960396,
]
SH_THREE = [
    -0.5900435899266435,
    2.890611442640554,
    -0.4570457994644658,
    0.3731763325901154,
    -0.4570457994644658,
    1.445305721320277,
    -0.5900435899266435,
]


def matmul3(left, right):
    return [
        [
            left[i][0] * right[0][j] + left[i][1] * right[1][j] + left[i][2] * right[2][j]
            for j in range(3)
        ]
        for i in range(3)
    ]


def view_of(cam_ref, view):
    values = []
    for k in range(6):
        value = jnp.zeros((8, 128), F32)
        for c in range(N_CAM):
            for p in range(2):
                value = jnp.where(view == c * 2 + p, cam_ref[p, c, k], value)
        values.append(value)
    cos_a, sin_a = jnp.cos(values[0]), jnp.sin(values[0])
    cos_b, sin_b = jnp.cos(values[1]), jnp.sin(values[1])
    cos_c, sin_c = jnp.cos(values[2]), jnp.sin(values[2])
    rotate = [
        [cos_c * cos_b, cos_c * sin_b * sin_a - sin_c * cos_a, cos_c * sin_b * cos_a + sin_c * sin_a],
        [sin_c * cos_b, sin_c * sin_b * sin_a + cos_c * cos_a, sin_c * sin_b * cos_a - cos_c * sin_a],
        [-sin_b, cos_b * sin_a, cos_b * cos_a],
    ]
    offset = [values[3], values[4], 6.0 + values[5]]
    anchor = [
        -(rotate[0][j] * offset[0] + rotate[1][j] * offset[1] + rotate[2][j] * offset[2])
        for j in range(3)
    ]
    return [rotate[i][j] for i in range(3) for j in range(3)] + offset + anchor


def covariance_of(raw):
    quat_norm = jnp.sqrt(raw[3] * raw[3] + raw[4] * raw[4] + raw[5] * raw[5] + raw[6] * raw[6])
    per_norm = 1.0 / quat_norm
    qw, qx, qy, qz = (raw[3] * per_norm, raw[4] * per_norm, raw[5] * per_norm, raw[6] * per_norm)
    spin = [
        [1.0 - 2.0 * (qy * qy + qz * qz), 2.0 * (qx * qy - qw * qz), 2.0 * (qx * qz + qw * qy)],
        [2.0 * (qx * qy + qw * qz), 1.0 - 2.0 * (qx * qx + qz * qz), 2.0 * (qy * qz - qw * qx)],
        [2.0 * (qx * qz - qw * qy), 2.0 * (qy * qz + qw * qx), 1.0 - 2.0 * (qx * qx + qy * qy)],
    ]
    squares = [jnp.exp(2.0 * raw[k]) for k in range(3)]
    return [
        spin[i][0] * spin[j][0] * squares[0]
        + spin[i][1] * spin[j][1] * squares[1]
        + spin[i][2] * spin[j][2] * squares[2]
        for i, j in ((0, 0), (0, 1), (0, 2), (1, 1), (1, 2), (2, 2))
    ]


def screen_of(point, cov, colors, view):
    rotate = [view[0:3], view[3:6], view[6:9]]
    offset, anchor = view[9:12], view[12:15]
    viewed = [
        rotate[i][0] * point[0] + rotate[i][1] * point[1] + rotate[i][2] * point[2] + offset[i]
        for i in range(3)
    ]
    toward = [point[j] - anchor[j] for j in range(3)]
    length = jnp.sqrt(toward[0] * toward[0] + toward[1] * toward[1] + toward[2] * toward[2])
    per_length = 1.0 / length
    ux, uy, uz = (toward[0] * per_length, toward[1] * per_length, toward[2] * per_length)
    world = [[cov[0], cov[1], cov[2]], [cov[1], cov[3], cov[4]], [cov[2], cov[4], cov[5]]]
    half_way = matmul3(rotate, world)

    def seen(a, b):
        return (
            half_way[a][0] * rotate[b][0] + half_way[a][1] * rotate[b][1] + half_way[a][2] * rotate[b][2]
        )

    c00, c01, c02 = seen(0, 0), seen(0, 1), seen(0, 2)
    c11, c12, c22 = seen(1, 1), seen(1, 2), seen(2, 2)
    inverse = 1.0 / viewed[2]
    j_main = FOCAL * inverse
    j_side_x = -j_main * viewed[0] * inverse
    j_side_y = -j_main * viewed[1] * inverse
    s_xx = j_main * j_main * c00 + 2.0 * j_main * j_side_x * c02 + j_side_x * j_side_x * c22 + 0.3
    s_xy = (
        j_main * j_main * c01
        + j_main * j_side_y * c02
        + j_side_x * j_main * c12
        + j_side_x * j_side_y * c22
    )
    s_yy = j_main * j_main * c11 + 2.0 * j_main * j_side_y * c12 + j_side_y * j_side_y * c22 + 0.3
    per_det = 1.0 / (s_xx * s_yy - s_xy * s_xy)
    xx, yy, zz = (ux * ux, uy * uy, uz * uz)
    basis = [
        None,
        -SH_ONE * uy,
        SH_ONE * uz,
        -SH_ONE * ux,
        SH_TWO[0] * ux * uy,
        SH_TWO[1] * uy * uz,
        SH_TWO[2] * (2.0 * zz - xx - yy),
        SH_TWO[3] * ux * uz,
        SH_TWO[4] * (xx - yy),
        SH_THREE[0] * uy * (3.0 * xx - yy),
        SH_THREE[1] * ux * uy * uz,
        SH_THREE[2] * uy * (4.0 * zz - xx - yy),
        SH_THREE[3] * uz * (2.0 * zz - 3.0 * xx - 3.0 * yy),
        SH_THREE[4] * ux * (4.0 * zz - xx - yy),
        SH_THREE[5] * uz * (xx - yy),
        SH_THREE[6] * ux * (xx - 3.0 * yy),
    ]
    channels = []
    for channel in range(3):
        total = 0.5 + SH_ZERO * colors[channel]
        for k in range(1, 16):
            total = total + basis[k] * colors[3 * k + channel]
        channels.append(total)
    return [
        j_main * viewed[0] + 2048.0,
        j_main * viewed[1] + 1024.0,
        s_yy * per_det,
        -s_xy * per_det,
        s_xx * per_det,
    ] + channels


def sigmoid(value):
    return 1.0 / (1.0 + jnp.exp(-value))


def split(value):
    high = value.astype(BF16)
    rest = value - high.astype(F32)
    mid = rest.astype(BF16)
    low = (rest - mid.astype(F32)).astype(BF16)
    return high, mid, low


def pick(chooser, value):
    high, mid, low = split(value)
    return (
        jnp.dot(chooser, high, preferred_element_type=F32)
        + jnp.dot(chooser, mid, preferred_element_type=F32)
    ) + jnp.dot(chooser, low, preferred_element_type=F32)


def pick_two(chooser, value):
    high = value.astype(BF16)
    mid = (value - high.astype(F32)).astype(BF16)
    return jnp.dot(chooser, high, preferred_element_type=F32) + jnp.dot(chooser, mid, preferred_element_type=F32)


def turn(value, lanes):
    lanes = lanes % 128
    return value if lanes == 0 else pltpu.roll(value, lanes, 1)


def spread_of(first):
    lane = lax.broadcasted_iota(jnp.int32, (128, 256), 1)
    row = lax.broadcasted_iota(jnp.int32, (128, 256), 0)
    return jnp.where(row == (first + lane // 128) * 16 + lax.rem(lane, 16), 1.0, 0.0).astype(BF16)


def expand(refs, flat, wide):
    flat[56:64, :] = jnp.zeros((8, 1024), F32)
    start = 0
    for ref in refs:
        flat[start : start + ref.shape[0], :] = ref[...]
        start += ref.shape[0]
    parts = split(jnp.concatenate([flat[:, j * 128 : (j + 1) * 128] for j in range(8)], axis=0))
    for i in range(0, 8, 2):
        spread = spread_of(i)
        value = (
            jnp.dot(parts[0], spread, preferred_element_type=F32)
            + jnp.dot(parts[1], spread, preferred_element_type=F32)
        ) + jnp.dot(parts[2], spread, preferred_element_type=F32)
        wide[:, i, :] = value[:, 0:128]
        wide[:, i + 1, :] = value[:, 128:256]


def project_chunk(chunk, wide, view_ref, out):
    view = [view_ref[k] for k in range(15)]
    raw = [wide[chunk * 64 + k] for k in range(59)]
    record = screen_of(raw[0:3], covariance_of(raw[3:10]), raw[11:], view)
    slot = lax.broadcasted_iota(jnp.int32, (8, 128), 1) // 16
    rows = pl.ds(pl.multiple_of(chunk * 8, 8), 8)
    for v in range(8):
        value = turn(record[0], -v * 16)
        for k in range(1, 8):
            value = jnp.where(slot == k, turn(record[k], (k - v) * 16), value)
        out[v, rows, :] = value
    out[8, rows, :] = sigmoid(raw[10])


def place():
    return lax.axis_index("cam"), lax.axis_index("tile")


def across(c, t, i):
    index = lax.rem(c * 4 + t // 16 + i, 16)
    return (index // 4, lax.rem(index, 4) * 16 + lax.rem(t, 16))


def along(c, t, i):
    return (c, (t // 16) * 16 + lax.rem(lax.rem(t, 16) + i, 16))


def greet(c, t):
    barrier = pltpu.get_barrier_semaphore()

    def hail(i, carry):
        pl.semaphore_signal(barrier, inc=1, device_id=along(c, t, i), device_id_type=MESH)
        pl.semaphore_signal(barrier, inc=1, device_id=across(c, t, i), device_id_type=MESH)
        return carry

    lax.fori_loop(1, 16, hail, 0)
    return barrier


def send_rows(src, dst, c, t, send, recv):
    me = c * N_TILE + t

    def one(i, carry):
        to = lax.rem(me + i, N_DEV)
        pltpu.make_async_remote_copy(
            src_ref=src.at[to],
            dst_ref=dst.at[me],
            send_sem=send,
            recv_sem=recv,
            device_id=(to // N_TILE, lax.rem(to, N_TILE)),
            device_id_type=MESH,
        ).start()
        return carry

    lax.fori_loop(1, N_DEV, one, 0, unroll=5)


def wait_rows(src, dst, send, recv):
    most = pl.ds(0, N_DEV - 1)
    pltpu.make_async_copy(src.at[most], src.at[most], send).wait()
    pltpu.make_async_copy(dst.at[most], dst.at[most], recv).wait()


def chooser_of(table, g):
    wanted = table[g * N_TILE : (g + 1) * N_TILE, 0, :]
    lane = lax.broadcasted_iota(jnp.int32, (64, 128), 1)
    return jnp.where(wanted == lax.rem(lane, 64), 1.0, 0.0)


def main_kernel(
    place_ref,
    count_ref,
    cam,
    pos,
    scl,
    rot,
    opa,
    col,
    fetch,
    lists,
    target,
    table,
    back_0,
    back_1,
    mine,
    flat,
    wide,
    view_ref,
    records,
    out_0,
    out_1,
    data_0,
    data_1,
    grad_0,
    grad_1,
    chosen,
    givers,
    spots,
    cols,
    alpha_ref,
    through_ref,
    lost,
    send_a,
    recv_a,
    send_b,
    recv_b,
    send_c,
    recv_c,
    send_d,
    recv_d,
    send_e,
    recv_e,
    send_f,
    recv_f,
    own_a,
    own_c,
    own_d,
    own_e,
    own_f,
):
    c, t = place()
    me = c * N_TILE + t
    barrier = greet(c, t)
    block = [fetch[p, 0, 0:1, 0:1] // 16 for p in range(2)]
    half = lax.broadcasted_iota(jnp.int32, (1, 128), 1) < 64
    mine[0, :, :] = jnp.where(half, jnp.broadcast_to(block[0], (1, 128)), jnp.broadcast_to(block[1], (1, 128)))
    for k, value in enumerate(view_of(cam, lax.broadcasted_iota(jnp.int32, (8, 128), 1) // 16)):
        view_ref[k] = value
    expand((pos, scl, rot, opa, col), flat, wide)

    def step(chunk, carry):
        project_chunk(chunk, wide, view_ref, records)
        return carry

    local = pltpu.make_async_copy(mine.at[0], table.at[me], own_a)
    local.start()
    pl.semaphore_wait(barrier, 30)

    def first(i, carry):
        pltpu.make_async_remote_copy(
            src_ref=mine.at[0],
            dst_ref=table.at[me],
            send_sem=send_a,
            recv_sem=recv_a,
            device_id=along(c, t, i),
            device_id_type=MESH,
        ).start()
        return carry

    lax.fori_loop(1, 16, first, 0)
    lax.fori_loop(0, 8, step, 0)
    local.wait()
    some = pl.ds(0, 15)
    pltpu.make_async_copy(table.at[some], table.at[some], send_a).wait()
    pltpu.make_async_copy(table.at[some], table.at[some], recv_a).wait()
    line = pl.ds(c * N_TILE + (t // 16) * 16, 16)

    def second(i, carry):
        pltpu.make_async_remote_copy(
            src_ref=table.at[line],
            dst_ref=table.at[line],
            send_sem=send_b,
            recv_sem=recv_b,
            device_id=across(c, t, i),
            device_id_type=MESH,
        ).start()
        return carry

    lax.fori_loop(1, 16, second, 0)
    for p in range(2):
        prepare(p, fetch, lists, chosen, givers, spots)
    most = pl.ds(0, 240)
    pltpu.make_async_copy(table.at[most], table.at[most], send_b).wait()
    pltpu.make_async_copy(table.at[most], table.at[most], recv_b).wait()

    lane = lax.broadcasted_iota(jnp.int32, (64, 128), 1)
    opacity = records[8]
    opacity = [jnp.where(lane // 16 == p, opacity, 0.0) for p in range(2)]
    none = jnp.zeros((64, 128), F32)
    for g in range(N_CAM):
        chooser = chooser_of(table, g).astype(BF16)
        upper = jnp.concatenate([records[2 * g], opacity[0], none], axis=1)
        lower = jnp.concatenate([none, opacity[1], records[2 * g + 1]], axis=1)
        value = pick(chooser, jnp.concatenate([upper, lower], axis=0))
        here = pl.ds(g * N_TILE, N_TILE)
        out_0[here, 0, :] = value[:, 0:128]
        out_0[here, 1, :] = value[:, 128:256]
        out_1[here, 0, :] = value[:, 256:384]
    local_0 = pltpu.make_async_copy(out_0.at[me], data_0.at[me], own_c)
    local_0.start()
    send_rows(out_0, data_0, c, t, send_c, recv_c)
    local_1 = pltpu.make_async_copy(out_1.at[me], data_1.at[me], own_d)
    local_1.start()
    send_rows(out_1, data_1, c, t, send_d, recv_d)
    local_0.wait()
    wait_rows(out_0, data_0, send_c, recv_c)
    opacity = data_0[:, 1, :]
    shared = (place_ref, count_ref, chosen, givers, spots, target, cols, alpha_ref, through_ref, lost)
    given_0, given_o = render(0, data_0[:, 0, :], opacity, *shared)
    grad_0[:, 0, :] = given_0
    local_0 = pltpu.make_async_copy(grad_0.at[me], back_0.at[me], own_e)
    local_0.start()
    send_rows(grad_0, back_0, c, t, send_e, recv_e)
    local_1.wait()
    wait_rows(out_1, data_1, send_d, recv_d)
    grad_1[:, 1, :] = given_o
    given_1, given_o = render(1, data_1[:, 0, :], opacity, *shared)
    grad_1[:, 0, :] = given_1
    grad_1[:, 1, :] = grad_1[:, 1, :] + given_o
    local_1 = pltpu.make_async_copy(grad_1.at[me], back_1.at[me], own_f)
    local_1.start()
    send_rows(grad_1, back_1, c, t, send_f, recv_f)
    local_0.wait()
    wait_rows(grad_0, back_0, send_e, recv_e)
    local_1.wait()
    wait_rows(grad_1, back_1, send_f, recv_f)


def prepare(p, fetch, lists, chosen, givers, spots):
    wide = lax.broadcasted_iota(jnp.int32, (LIST, N_DEV), 1)
    tall = lax.broadcasted_iota(jnp.int32, (LIST, N_DEV), 0)
    listed = jnp.broadcast_to(lists[p], (LIST, N_DEV)).astype(F32)
    slot = jnp.sum(jnp.where(wide == lax.rem(tall, 8) * 32 + tall // 8, listed, 0.0), axis=1, keepdims=True)
    slot = slot.astype(jnp.int32)
    chooser = jnp.where(wide == slot // 8, 1.0, 0.0)
    givers[p] = chooser.T.astype(BF16)
    chooser = chooser.astype(BF16)
    chosen[p] = chooser
    within = jnp.concatenate([lax.rem(fetch[p, g], 16).astype(F32) for g in range(N_CAM)], axis=1).astype(BF16)
    near = lax.dot_general(chooser, within, (((1,), (1,)), ((), ())), preferred_element_type=F32)
    eight = lax.broadcasted_iota(jnp.int32, near.shape, 1)
    column = jnp.sum(jnp.where(eight == lax.rem(slot, 8), near, 0.0), axis=1, keepdims=True)
    spots[p] = jnp.broadcast_to(column, (LIST, 128)).astype(jnp.int32)


def before_of(run):
    row = lax.broadcasted_iota(jnp.int32, (8, 128), 0)
    for s in (1, 2, 4):
        run = run * jnp.where(row >= s, pltpu.roll(run, s, 0), 1.0)
    return jnp.where(row >= 1, pltpu.roll(run, 1, 0), 1.0)


def after_of(run):
    row = lax.broadcasted_iota(jnp.int32, (8, 128), 0)
    for s in (1, 2, 4):
        run = run + jnp.where(row < 8 - s, pltpu.roll(run, 8 - s, 0), 0.0)
    return jnp.where(row < 7, pltpu.roll(run, 7, 0), 0.0)


def render(p, data, opacity, place_ref, count_ref, chosen, givers, spots, target, cols, alpha_ref, through_ref, lost):
    lane_b = lax.broadcasted_iota(jnp.int32, (BLK, 128), 1)
    row_b = lax.broadcasted_iota(jnp.int32, (BLK, 128), 0)
    lane_1 = lax.broadcasted_iota(jnp.int32, (1, 128), 1)
    blocks, parts = LIST // BLK, BLK // 8
    picked = pick(chosen[p], jnp.concatenate([data, opacity], axis=1))
    spot = spots[p]
    for k in range(9):
        source, first = (picked[:, 128:256], p * 16) if k == 8 else (picked[:, 0:128], k * 16)
        cols[k] = jnp.take_along_axis(source, spot + first, axis=1)

    tile = place_ref[p]
    count = count_ref[p]
    left = (lax.rem(tile, 256) * 16).astype(F32) + 0.5
    top = ((tile // 256) * 16).astype(F32) + 0.5
    px = left + lax.rem(lane_1, 16).astype(F32)
    py = [top + ((lane_1 + h * 128) // 16).astype(F32) for h in range(2)]

    def ahead(b, carry):
        rows = pl.ds(pl.multiple_of(b * BLK, BLK), BLK)
        u, v, ca, cb, cc = [cols[k, rows, :] for k in range(5)]
        shade = [cols[k, rows, :] for k in (5, 6, 7)]
        o = cols[8, rows, :]
        live = lax.rem(row_b, 8) * 32 + row_b // 8 + b * parts < count
        dx = px - u
        dxx = ca * dx * dx
        result = []
        for h in range(2):
            run, shown = carry[h][0], list(carry[h][1:])
            dy = py[h] - v
            quad = dxx + 2.0 * cb * dx * dy + cc * dy * dy
            alpha = jnp.where(live, o * jnp.exp(-0.5 * quad), 0.0)
            alpha_ref[h, rows, :] = alpha
            keep = 1.0 - alpha
            before = []
            for n in range(parts):
                before.append(run)
                run = run * keep[8 * n : 8 * n + 8]
            before = jnp.concatenate(before, axis=0)
            through_ref[h, rows, :] = before
            weight = alpha * before
            for k in range(3):
                value = shade[k] * weight
                for n in range(parts):
                    shown[k] = shown[k] + value[8 * n : 8 * n + 8]
            result.append((run, *shown))
        return tuple(result)

    one, zero = jnp.ones((8, 128), F32), jnp.zeros((8, 128), F32)
    state = lax.fori_loop(0, blocks, ahead, ((one, zero, zero, zero),) * 2)
    ahead_of, miss, behind = [], [], []
    for h in range(2):
        prefix = before_of(state[h][0])
        parts_of = [prefix * state[h][1 + k] for k in range(3)]
        gap = [
            jnp.sum(parts_of[k], axis=0, keepdims=True) - target[p, k, :, h * 128 : (h + 1) * 128]
            for k in range(3)
        ]
        ahead_of.append(jnp.concatenate([prefix] * parts, axis=0))
        miss.append(gap)
        behind.append(after_of(gap[0] * parts_of[0] + gap[1] * parts_of[1] + gap[2] * parts_of[2]))

    def back(i, carry):
        b = blocks - 1 - i
        rows = pl.ds(pl.multiple_of(b * BLK, BLK), BLK)
        u, v, ca, cb, cc = [cols[k, rows, :] for k in range(5)]
        shade = [cols[k, rows, :] for k in (5, 6, 7)]
        o = cols[8, rows, :]
        dx = px - u
        sums = [0.0] * 9
        result = []
        for h in range(2):
            alpha = alpha_ref[h, rows, :]
            before = through_ref[h, rows, :] * ahead_of[h]
            dy = py[h] - v
            weight = alpha * before
            pull = shade[0] * miss[h][0] + shade[1] * miss[h][1] + shade[2] * miss[h][2]
            value = pull * weight
            run = carry[h]
            after = []
            for n in reversed(range(parts)):
                after.insert(0, run)
                run = run + value[8 * n : 8 * n + 8]
            result.append(run)
            after = jnp.concatenate(after, axis=0)
            slope = (before * pull - after / (1.0 - alpha)) * alpha
            tilt_x, tilt_y = slope * dx, slope * dy
            terms = [tilt_x, tilt_y, tilt_x * dx, tilt_x * dy, tilt_y * dy, slope]
            terms = terms + [weight * miss[h][k] for k in range(3)]
            sums = [x + y for x, y in zip(sums, terms)]
        m_x, m_y, m_xx, m_xy, m_yy, m_0, *g_shade = [jnp.sum(x, axis=1, keepdims=True) for x in sums]
        grads = [ca * m_x + cb * m_y, cb * m_x + cc * m_y, -0.5 * m_xx, -m_xy, -0.5 * m_yy] + g_shade
        spot_b = spots[p, rows, :]
        value = jnp.zeros((BLK, 128), F32)
        for k in range(8):
            value = jnp.where(lane_b == spot_b + k * 16, jnp.broadcast_to(grads[k], (BLK, 128)), value)
        lost[rows, 0:128] = value
        lost[rows, 128:256] = jnp.where(lane_b == spot_b + p * 16, m_0 / o, 0.0)
        return tuple(result)

    lax.fori_loop(0, blocks, back, tuple(behind))
    given = pick_two(givers[p], lost[...])
    return given[:, 0:128], given[:, 128:256]


def gradient_kernel(
    cam, pos, scl, rot, opa, col, table, back_0, back_1, g_pos, g_scl, g_rot, g_opa, g_col, raw, view_ref, cot, total
):
    row = lax.broadcasted_iota(jnp.int32, (8, 128), 0)
    lane = lax.broadcasted_iota(jnp.int32, (8, 128), 1)
    for k, value in enumerate(view_of(cam, row)):
        view_ref[k] = value
    start = 0
    for ref in (pos, scl, rot, opa, col):
        for j in range(8):
            raw[start : start + ref.shape[0], j, :] = ref[:, j * 128 : (j + 1) * 128]
        start += ref.shape[0]

    def fold(value, first):
        out = jnp.zeros((8, 128), F32)
        for j in range(8):
            part = jnp.take_along_axis(value[8 * j : 8 * j + 8], first + lax.rem(lane, 16), axis=1)
            part = jnp.take_along_axis(part, lane // 16, axis=0)
            out = jnp.where(row == j, part, out)
        return out

    opacity = jnp.zeros((8, 128), F32)
    for g in range(N_CAM):
        chooser = chooser_of(table, g).T.astype(BF16)
        here = pl.ds(g * N_TILE, N_TILE)
        sent = jnp.concatenate([back_0[here, 0, :], back_1[here, 1, :], back_1[here, 0, :]], axis=1)
        value = pick_two(chooser, sent)
        for p in range(2):
            part = value[p * 64 : p * 64 + 64, p * 256 : p * 256 + 128]
            for v in range(8):
                cot[2 * g + p, v] = fold(part, v * 16)
            opacity = opacity + fold(value[p * 64 : p * 64 + 64, 128:256], p * 16)
    for k in range(57):
        total[k] = jnp.zeros((8, 128), F32)
    shape_raw = [raw[k] for k in range(3, 10)]
    for k, value in enumerate(covariance_of(shape_raw)):
        cot[8, k] = value

    def step(v, carry):
        view = [view_ref[k, pl.ds(v, 1), :] for k in range(15)]
        point = [raw[k] for k in range(3)]
        cov = [cot[8, k] for k in range(6)]
        colors = [raw[11 + k] for k in range(48)]
        _, pull = jax.vjp(lambda a, b, d: screen_of(a, b, d, view), point, cov, colors)
        grads = pull([cot[v, k] for k in range(8)])
        for k, value in enumerate(grads[0] + grads[1] + grads[2]):
            total[k] = total[k] + value
        return carry

    lax.fori_loop(0, 8, step, 0)
    _, pull = jax.vjp(covariance_of, [raw[k] for k in range(3, 10)])
    (shape_grads,) = pull([total[3 + k] for k in range(6)])
    for k in range(7):
        total[57 + k] = shape_grads[k]
    o = sigmoid(raw[10])
    total[3] = opacity * o * (1.0 - o)
    for j in range(8):
        here = pl.ds(j * 128, 128)
        g_pos[:, here] = total[0:3, j, :]
        g_scl[:, here] = total[57:60, j, :]
        g_rot[:, here] = total[60:64, j, :]
        g_opa[:, here] = total[3:4, j, :]
        g_col[:, here] = total[9:57, j, :]


VMEM = pl.BlockSpec(memory_space=pltpu.VMEM)
SMEM = pl.BlockSpec(memory_space=pltpu.SMEM)
DMA = pltpu.SemaphoreType.DMA


def shape(*dims, dtype=F32):
    return jax.ShapeDtypeStruct(dims, dtype)


def body(
    positions,
    log_scales,
    rotations,
    opacities,
    colors,
    cameras,
    targets,
    tile_ids,
    tile_counts,
    tile_lists,
    fetch_ids,
):
    params = (positions, log_scales, rotations, opacities.reshape(1, 1024), colors)
    single, double = pltpu.VMEM((N_DEV, 1, 128), F32), pltpu.VMEM((N_DEV, 2, 128), F32)
    table, back_0, back_1 = pl.pallas_call(
        main_kernel,
        out_shape=(shape(N_DEV, 1, 128, dtype=jnp.int32), shape(N_DEV, 1, 128), shape(N_DEV, 2, 128)),
        in_specs=[SMEM] * 3 + [VMEM] * 8,
        out_specs=(VMEM,) * 3,
        scratch_shapes=[
            pltpu.VMEM((1, 1, 128), jnp.int32),
            pltpu.VMEM((64, 1024), F32),
            pltpu.VMEM((512, 8, 128), F32),
            pltpu.VMEM((15, 8, 128), F32),
            pltpu.VMEM((9, 64, 128), F32),
            double,
            single,
            double,
            single,
            single,
            double,
            pltpu.VMEM((2, LIST, N_DEV), BF16),
            pltpu.VMEM((2, N_DEV, LIST), BF16),
            pltpu.VMEM((2, LIST, 128), jnp.int32),
            pltpu.VMEM((9, LIST, 128), F32),
            pltpu.VMEM((2, LIST, 128), F32),
            pltpu.VMEM((2, LIST, 128), F32),
            pltpu.VMEM((LIST, 2 * 128), F32),
        ]
        + [DMA] * 17,
        compiler_params=pltpu.CompilerParams(collective_id=0, has_side_effects=True),
    )(
        tile_ids.reshape(2),
        tile_counts.reshape(2),
        cameras,
        *params,
        fetch_ids.reshape(2, N_CAM, N_TILE, 8).transpose(0, 1, 3, 2),
        tile_lists.reshape(2, 1, LIST),
        targets.reshape(2, 3, 1, PIX),
    )

    g_pos, g_scl, g_rot, g_opa, g_col = pl.pallas_call(
        gradient_kernel,
        out_shape=tuple(shape(n, 1024) for n in (3, 3, 4, 1, 48)),
        in_specs=[SMEM] + [VMEM] * 8,
        out_specs=(VMEM,) * 5,
        scratch_shapes=[
            pltpu.VMEM((59, 8, 128), F32),
            pltpu.VMEM((15, 8, 128), F32),
            pltpu.VMEM((9, 8, 8, 128), F32),
            pltpu.VMEM((64, 8, 128), F32),
        ],
    )(cameras, *params, table, back_0, back_1)
    return g_pos, g_scl, g_rot, g_opa.reshape(1024), g_col


def solution(mesh):
    return jax.shard_map(
        body,
        mesh=mesh,
        in_specs=(
            P(None, ("cam", "tile")),
            P(None, ("cam", "tile")),
            P(None, ("cam", "tile")),
            P(("cam", "tile")),
            P(None, ("cam", "tile")),
            P(),
            P(None, "cam", "tile", None, None),
            P(None, "cam", "tile"),
            P(None, "cam", "tile"),
            P(None, "cam", "tile", None),
            P(None, "cam", "tile", None, None, None),
        ),
        out_specs=(
            P(None, ("cam", "tile")),
            P(None, ("cam", "tile")),
            P(None, ("cam", "tile")),
            P(("cam", "tile")),
            P(None, ("cam", "tile")),
        ),
        check_vma=False,
    )
```

time: 67 us -> 57.9 us (0.86)
  Pallas kernels: 63 us -> 57.1 us
  local copies, waits for them, and re-layouts: 3.04 us -> 0 us
    pallas_call x1, Pallas kernels: 9.57 us -> 4.53 us  [body(): pl.pallas_call(gradient_kernel, out_shape=tuple((shape(n, 1024) for n in...]
    another operation x2 -> x0, local copies, waits for them, and re-layouts: 1.44 us -> none  [the longest x1 0.84 us: body(): lists.reshape(2, LIST, 1)]
    pallas_call x1, Pallas kernels: 53.5 us -> 52.6 us  [body(): pl.pallas_call(main_kernel, out_shape=(shape(N_DEV, 1, 128, dtype=jnp.int...]
    unnamed x10 -> x0, local copies, waits for them, and re-layouts: 0.81 us -> none
where the time goes in v2:
time: 57.9 us; the launch traced here: 57.8 us
  Pallas kernels  57.1 us (99%)
  between operations  0.64 us (1%)
    pallas_call x1, Pallas kernels, body(): pl.pallas_call(main_kernel, out_shape=(shape(N_DEV, 1, 128, dtype=jnp.int...  52.6 us
    pallas_call x1, Pallas kernels, body(): pl.pallas_call(gradient_kernel, out_shape=tuple((shape(n, 1024) for n in...  4.53 us

profile of v2, /device:TPU:1, one launch (start us, length us, event | category | flops | bytes accessed | tf_op | source)
XLA Modules:
  0.0 57.8 jit_solution(670237401360195367)
XLA Ops:
  0.6 52.6 %shard_map.146 = (s32[256,1,128]{2,1,0:T(1,128)}, f32[256,1,128]{2,1,0:T(1,128)}, f32[256,2,128]{2,1,0:T(2,128)}) custom-call(s32[2]{0:T(128)} %bitcast.14, s32[2]{0:T(128)} %bitcast.15, f32[2,4,6]{2,1,0:T(4,128)} %cam.3, f32[3,1024]{1,0:T(4,128)} %pos.3, f32[3,1024]{1,0:T(4,128)} %scl.3, f32[4,1024]{1,0:T(4,128)} %rot.3, f32[1,1024]{1,0:T(1,128)} %bitcast.10, ...), custom_call_target="tpu_custom_call" | custom-call | tf_op jit(solution)/shard_map/pallas_call | solution.py:651
  53.2 4.5 %shard_map.147 = (f32[3,1024]{1,0:T(4,128)}, f32[3,1024]{1,0:T(4,128)}, f32[4,1024]{1,0:T(4,128)}, f32[1,1024]{1,0:T(1,128)}, f32[48,1024]{1,0:T(8,128)}) custom-call(f32[2,4,6]{2,1,0:T(4,128)} %cam.3, f32[3,1024]{1,0:T(4,128)} %pos.3, f32[3,1024]{1,0:T(4,128)} %scl.3, f32[4,1024]{1,0:T(4,128)} %rot.3, f32[1,1024]{1,0:T(1,128)} %bitcast.11, f32[48,1024]{1,0:T(8,128)} %col.3, ...), custom_call_target="tpu_custom_call" | custom-call | tf_op jit(solution)/shard_map/pallas_call | solution.py:688

commit v3 on v2

--- a/solution.py
+++ b/solution.py
@@ -262,6 +262,40 @@
     lax.fori_loop(1, N_DEV, one, 0, unroll=5)
 
 
+def send_plane(src, dst, c, t, send, recv):
+    def one(i, carry):
+        to = lax.rem(t + i, N_TILE)
+        pltpu.make_async_remote_copy(
+            src_ref=src.at[to],
+            dst_ref=dst.at[t],
+            send_sem=send,
+            recv_sem=recv,
+            device_id=(c, to),
+            device_id_type=MESH,
+        ).start()
+        return carry
+
+    lax.fori_loop(1, N_TILE, one, 0, unroll=3)
+
+
+def send_mates(src, dst, c, t, send, recv):
+    for i in range(1, N_CAM):
+        pltpu.make_async_remote_copy(
+            src_ref=src,
+            dst_ref=dst.at[c],
+            send_sem=send,
+            recv_sem=recv,
+            device_id=(lax.rem(c + i, N_CAM), t),
+            device_id_type=MESH,
+        ).start()
+
+
+def wait_some(src, dst, count, send, recv):
+    some = pl.ds(0, count)
+    pltpu.make_async_copy(src.at[some], src.at[some], send).wait()
+    pltpu.make_async_copy(dst.at[some], dst.at[some], recv).wait()
+
+
 def wait_rows(src, dst, send, recv):
     most = pl.ds(0, N_DEV - 1)
     pltpu.make_async_copy(src.at[most], src.at[most], send).wait()
@@ -287,22 +321,26 @@
     lists,
     target,
     table,
-    back_0,
-    back_1,
+    back,
+    back_o,
     mine,
     flat,
     wide,
     view_ref,
     records,
-    out_0,
-    out_1,
-    data_0,
-    data_1,
-    grad_0,
-    grad_1,
+    out,
+    out_o,
+    data,
+    data_o,
+    grad,
+    grad_o,
+    mates,
+    came_o,
+    share,
     chosen,
     givers,
     spots,
+    spots_o,
     cols,
     alpha_ref,
     through_ref,
@@ -315,15 +353,21 @@
     recv_c,
     send_d,
     recv_d,
-    send_e,
-    recv_e,
-    send_f,
-    recv_f,
+    send_g,
+    recv_g,
+    send_h,
+    recv_h,
+    send_i,
+    recv_i,
+    send_j,
+    recv_j,
     own_a,
     own_c,
     own_d,
-    own_e,
-    own_f,
+    own_g,
+    own_h,
+    own_i,
+    own_j,
 ):
     c, t = place()
     me = c * N_TILE + t
@@ -356,6 +400,9 @@
 
     lax.fori_loop(1, 16, first, 0)
     lax.fori_loop(0, 8, step, 0)
+    local_o = pltpu.make_async_copy(records.at[8], mates.at[c], own_g)
+    local_o.start()
+    send_mates(records.at[8], mates, c, t, send_g, recv_g)
     local.wait()
     some = pl.ds(0, 15)
     pltpu.make_async_copy(table.at[some], table.at[some], send_a).wait()
@@ -375,55 +422,68 @@
 
     lax.fori_loop(1, 16, second, 0)
     for p in range(2):
-        prepare(p, fetch, lists, chosen, givers, spots)
+        prepare(p, fetch, lists, chosen, givers, spots, spots_o)
     most = pl.ds(0, 240)
     pltpu.make_async_copy(table.at[most], table.at[most], send_b).wait()
     pltpu.make_async_copy(table.at[most], table.at[most], recv_b).wait()
 
     lane = lax.broadcasted_iota(jnp.int32, (64, 128), 1)
-    opacity = records[8]
-    opacity = [jnp.where(lane // 16 == p, opacity, 0.0) for p in range(2)]
+    even = lax.rem(lane // 16, 2) == 0
+    local_o.wait()
+    wait_some(mates, mates, 3, send_g, recv_g)
+    opacity = mates[0]
+    for g in range(1, N_CAM):
+        opacity = jnp.where(lane // 32 == g, mates[g], opacity)
+    opacity = jnp.concatenate([jnp.where(even, opacity, 0.0), jnp.where(even, 0.0, opacity)], axis=0)
+    mine_rows = pl.ds(c * N_TILE, N_TILE)
+    chooser = jnp.where(table[mine_rows, 0, :] == lax.rem(lane, 64), 1.0, 0.0)
+    turned = chooser.T.astype(BF16)
+    out_o[:, 0, :] = pick(chooser.astype(BF16), opacity)
+    local_o = pltpu.make_async_copy(out_o.at[t], data_o.at[t], own_h)
+    local_o.start()
+    send_plane(out_o, data_o, c, t, send_h, recv_h)
     none = jnp.zeros((64, 128), F32)
     for g in range(N_CAM):
         chooser = chooser_of(table, g).astype(BF16)
-        upper = jnp.concatenate([records[2 * g], opacity[0], none], axis=1)
-        lower = jnp.concatenate([none, opacity[1], records[2 * g + 1]], axis=1)
+        upper = jnp.concatenate([records[2 * g], none], axis=1)
+        lower = jnp.concatenate([none, records[2 * g + 1]], axis=1)
         value = pick(chooser, jnp.concatenate([upper, lower], axis=0))
         here = pl.ds(g * N_TILE, N_TILE)
-        out_0[here, 0, :] = value[:, 0:128]
-        out_0[here, 1, :] = value[:, 128:256]
-        out_1[here, 0, :] = value[:, 256:384]
-    local_0 = pltpu.make_async_copy(out_0.at[me], data_0.at[me], own_c)
-    local_0.start()
-    send_rows(out_0, data_0, c, t, send_c, recv_c)
-    local_1 = pltpu.make_async_copy(out_1.at[me], data_1.at[me], own_d)
-    local_1.start()
-    send_rows(out_1, data_1, c, t, send_d, recv_d)
-    local_0.wait()
-    wait_rows(out_0, data_0, send_c, recv_c)
-    opacity = data_0[:, 1, :]
-    shared = (place_ref, count_ref, chosen, givers, spots, target, cols, alpha_ref, through_ref, lost)
-    given_0, given_o = render(0, data_0[:, 0, :], opacity, *shared)
-    grad_0[:, 0, :] = given_0
-    local_0 = pltpu.make_async_copy(grad_0.at[me], back_0.at[me], own_e)
-    local_0.start()
-    send_rows(grad_0, back_0, c, t, send_e, recv_e)
-    local_1.wait()
-    wait_rows(out_1, data_1, send_d, recv_d)
-    grad_1[:, 1, :] = given_o
-    given_1, given_o = render(1, data_1[:, 0, :], opacity, *shared)
-    grad_1[:, 0, :] = given_1
-    grad_1[:, 1, :] = grad_1[:, 1, :] + given_o
-    local_1 = pltpu.make_async_copy(grad_1.at[me], back_1.at[me], own_f)
-    local_1.start()
-    send_rows(grad_1, back_1, c, t, send_f, recv_f)
-    local_0.wait()
-    wait_rows(grad_0, back_0, send_e, recv_e)
-    local_1.wait()
-    wait_rows(grad_1, back_1, send_f, recv_f)
-
-
-def prepare(p, fetch, lists, chosen, givers, spots):
+        out[here, 0, :] = value[:, 0:128]
+        out[here, 1, :] = value[:, 128:256]
+    local = pltpu.make_async_copy(out.at[me], data.at[me], own_c)
+    local.start()
+    send_rows(out, data, c, t, send_c, recv_c)
+    local_o.wait()
+    wait_some(out_o, data_o, N_TILE - 1, send_h, recv_h)
+    local.wait()
+    wait_rows(out, data, send_c, recv_c)
+    shared = (place_ref, count_ref, chosen, givers, spots, spots_o, target, cols, alpha_ref, through_ref, lost)
+    for p in range(2):
+        opacity = jnp.concatenate([data_o[:, 0, :]] * N_CAM, axis=0)
+        given, given_o = render(p, data[:, p, :], opacity, *shared)
+        grad[:, p, :] = given
+        grad_o[:, 0, :] = given_o if p == 0 else grad_o[:, 0, :] + given_o
+    local_o = pltpu.make_async_copy(grad_o.at[t], came_o.at[t], own_i)
+    local_o.start()
+    send_plane(grad_o, came_o, c, t, send_i, recv_i)
+    local = pltpu.make_async_copy(grad.at[me], back.at[me], own_d)
+    local.start()
+    send_rows(grad, back, c, t, send_d, recv_d)
+    local_o.wait()
+    wait_some(grad_o, came_o, N_TILE - 1, send_i, recv_i)
+    both = pick_two(turned, came_o[:, 0, :])
+    share[...] = jnp.where(even, both[0:64], both[64:128])
+    local_o = pltpu.make_async_copy(share, back_o.at[c], own_j)
+    local_o.start()
+    send_mates(share, back_o, c, t, send_j, recv_j)
+    local_o.wait()
+    wait_some(back_o, back_o, 3, send_j, recv_j)
+    local.wait()
+    wait_rows(grad, back, send_d, recv_d)
+
+
+def prepare(p, fetch, lists, chosen, givers, spots, spots_o):
     wide = lax.broadcasted_iota(jnp.int32, (LIST, N_DEV), 1)
     tall = lax.broadcasted_iota(jnp.int32, (LIST, N_DEV), 0)
     listed = jnp.broadcast_to(lists[p], (LIST, N_DEV)).astype(F32)
@@ -437,7 +497,9 @@
     near = lax.dot_general(chooser, within, (((1,), (1,)), ((), ())), preferred_element_type=F32)
     eight = lax.broadcasted_iota(jnp.int32, near.shape, 1)
     column = jnp.sum(jnp.where(eight == lax.rem(slot, 8), near, 0.0), axis=1, keepdims=True)
-    spots[p] = jnp.broadcast_to(column, (LIST, 128)).astype(jnp.int32)
+    spot = jnp.broadcast_to(column, (LIST, 128)).astype(jnp.int32)
+    spots[p] = spot
+    spots_o[p] = spot + (slot // 512) * 32 + p * 16
 
 
 def before_of(run):
@@ -454,16 +516,18 @@
     return jnp.where(row < 7, pltpu.roll(run, 7, 0), 0.0)
 
 
-def render(p, data, opacity, place_ref, count_ref, chosen, givers, spots, target, cols, alpha_ref, through_ref, lost):
+def render(
+    p, data, opacity, place_ref, count_ref, chosen, givers, spots, spots_o, target, cols, alpha_ref, through_ref, lost
+):
     lane_b = lax.broadcasted_iota(jnp.int32, (BLK, 128), 1)
     row_b = lax.broadcasted_iota(jnp.int32, (BLK, 128), 0)
     lane_1 = lax.broadcasted_iota(jnp.int32, (1, 128), 1)
     blocks, parts = LIST // BLK, BLK // 8
     picked = pick(chosen[p], jnp.concatenate([data, opacity], axis=1))
     spot = spots[p]
-    for k in range(9):
-        source, first = (picked[:, 128:256], p * 16) if k == 8 else (picked[:, 0:128], k * 16)
-        cols[k] = jnp.take_along_axis(source, spot + first, axis=1)
+    for k in range(8):
+        cols[k] = jnp.take_along_axis(picked[:, 0:128], spot + k * 16, axis=1)
+    cols[8] = jnp.take_along_axis(picked[:, 128:256], spots_o[p], axis=1)
 
     tile = place_ref[p]
     count = count_ref[p]
@@ -551,16 +615,19 @@
         for k in range(8):
             value = jnp.where(lane_b == spot_b + k * 16, jnp.broadcast_to(grads[k], (BLK, 128)), value)
         lost[rows, 0:128] = value
-        lost[rows, 128:256] = jnp.where(lane_b == spot_b + p * 16, m_0 / o, 0.0)
+        lost[rows, 128:256] = jnp.where(lane_b == spots_o[p, rows, :], m_0 / o, 0.0)
         return tuple(result)
 
     lax.fori_loop(0, blocks, back, tuple(behind))
     given = pick_two(givers[p], lost[...])
-    return given[:, 0:128], given[:, 128:256]
+    by_tile = given[0:64, 128:256]
+    for g in range(1, N_CAM):
+        by_tile = by_tile + given[g * 64 : g * 64 + 64, 128:256]
+    return given[:, 0:128], by_tile
 
 
 def gradient_kernel(
-    cam, pos, scl, rot, opa, col, table, back_0, back_1, g_pos, g_scl, g_rot, g_opa, g_col, raw, view_ref, cot, total
+    cam, pos, scl, rot, opa, col, table, back, back_o, g_pos, g_scl, g_rot, g_opa, g_col, raw, view_ref, cot, total
 ):
     row = lax.broadcasted_iota(jnp.int32, (8, 128), 0)
     lane = lax.broadcasted_iota(jnp.int32, (8, 128), 1)
@@ -580,17 +647,18 @@
             out = jnp.where(row == j, part, out)
         return out
 
-    opacity = jnp.zeros((8, 128), F32)
+    own = lax.axis_index("cam") * 32
+    shared = (back_o[0] + back_o[1]) + (back_o[2] + back_o[3])
+    opacity = fold(shared, own) + fold(shared, own + 16)
     for g in range(N_CAM):
         chooser = chooser_of(table, g).T.astype(BF16)
         here = pl.ds(g * N_TILE, N_TILE)
-        sent = jnp.concatenate([back_0[here, 0, :], back_1[here, 1, :], back_1[here, 0, :]], axis=1)
+        sent = jnp.concatenate([back[here, 0, :], back[here, 1, :]], axis=1)
         value = pick_two(chooser, sent)
         for p in range(2):
-            part = value[p * 64 : p * 64 + 64, p * 256 : p * 256 + 128]
+            part = value[p * 64 : p * 64 + 64, p * 128 : p * 128 + 128]
             for v in range(8):
                 cot[2 * g + p, v] = fold(part, v * 16)
-            opacity = opacity + fold(value[p * 64 : p * 64 + 64, 128:256], p * 16)
     for k in range(57):
         total[k] = jnp.zeros((8, 128), F32)
     shape_raw = [raw[k] for k in range(3, 10)]
@@ -647,10 +715,14 @@
     fetch_ids,
 ):
     params = (positions, log_scales, rotations, opacities.reshape(1, 1024), colors)
-    single, double = pltpu.VMEM((N_DEV, 1, 128), F32), pltpu.VMEM((N_DEV, 2, 128), F32)
-    table, back_0, back_1 = pl.pallas_call(
+    whole, plane = pltpu.VMEM((N_DEV, 2, 128), F32), pltpu.VMEM((N_TILE, 1, 128), F32)
+    table, back, back_o = pl.pallas_call(
         main_kernel,
-        out_shape=(shape(N_DEV, 1, 128, dtype=jnp.int32), shape(N_DEV, 1, 128), shape(N_DEV, 2, 128)),
+        out_shape=(
+            shape(N_DEV, 1, 128, dtype=jnp.int32),
+            shape(N_DEV, 2, 128),
+            shape(N_CAM, 64, 128),
+        ),
         in_specs=[SMEM] * 3 + [VMEM] * 8,
         out_specs=(VMEM,) * 3,
         scratch_shapes=[
@@ -659,21 +731,25 @@
             pltpu.VMEM((512, 8, 128), F32),
             pltpu.VMEM((15, 8, 128), F32),
             pltpu.VMEM((9, 64, 128), F32),
-            double,
-            single,
-            double,
-            single,
-            single,
-            double,
+            whole,
+            plane,
+            whole,
+            plane,
+            whole,
+            plane,
+            pltpu.VMEM((N_CAM, 64, 128), F32),
+            plane,
+            pltpu.VMEM((64, 128), F32),
             pltpu.VMEM((2, LIST, N_DEV), BF16),
             pltpu.VMEM((2, N_DEV, LIST), BF16),
+            pltpu.VMEM((2, LIST, 128), jnp.int32),
             pltpu.VMEM((2, LIST, 128), jnp.int32),
             pltpu.VMEM((9, LIST, 128), F32),
             pltpu.VMEM((2, LIST, 128), F32),
             pltpu.VMEM((2, LIST, 128), F32),
             pltpu.VMEM((LIST, 2 * 128), F32),
         ]
-        + [DMA] * 17,
+        + [DMA] * 23,
         compiler_params=pltpu.CompilerParams(collective_id=0, has_side_effects=True),
     )(
         tile_ids.reshape(2),
@@ -696,7 +772,7 @@
             pltpu.VMEM((9, 8, 8, 128), F32),
             pltpu.VMEM((64, 8, 128), F32),
         ],
-    )(cameras, *params, table, back_0, back_1)
+    )(cameras, *params, table, back, back_o)
     return g_pos, g_scl, g_rot, g_opa.reshape(1024), g_col
 
 

time: 57.9 us -> 55.4 us (0.957)
  Pallas kernels: 57.1 us -> 54.7 us
    pallas_call x1, Pallas kernels: 52.6 us -> 50.3 us  [body(): pl.pallas_call(main_kernel, out_shape=(shape(N_DEV, 1, 128, dtype=jnp.int...]
where the time goes in v3:
time: 55.4 us; the launch traced here: 55.3 us
  Pallas kernels  54.7 us (99%)
  between operations  0.64 us (1%)
    pallas_call x1, Pallas kernels, body(): pl.pallas_call(main_kernel, out_shape=(shape(N_DEV, 1, 128, dtype=jnp.int...  50.3 us
    pallas_call x1, Pallas kernels, body(): pl.pallas_call(gradient_kernel, out_shape=tuple((shape(n, 1024) for n in...  4.35 us

profile of v3, /device:TPU:1, one launch (start us, length us, event | category | flops | bytes accessed | tf_op | source)
XLA Modules:
  0.0 55.3 jit_solution(12608955837387712382)
XLA Ops:
  0.6 50.3 %shard_map.146 = (s32[256,1,128]{2,1,0:T(1,128)}, f32[256,2,128]{2,1,0:T(2,128)}, f32[4,64,128]{2,1,0:T(8,128)}) custom-call(s32[2]{0:T(128)} %bitcast.14, s32[2]{0:T(128)} %bitcast.15, f32[2,4,6]{2,1,0:T(4,128)} %cam.3, f32[3,1024]{1,0:T(4,128)} %pos.3, f32[3,1024]{1,0:T(4,128)} %scl.3, f32[4,1024]{1,0:T(4,128)} %rot.3, f32[1,1024]{1,0:T(1,128)} %bitcast.10, ...), custom_call_target="tpu_custom_call" | custom-call | tf_op jit(solution)/shard_map/pallas_call | solution.py:719
  51.0 4.3 %shard_map.147 = (f32[3,1024]{1,0:T(4,128)}, f32[3,1024]{1,0:T(4,128)}, f32[4,1024]{1,0:T(4,128)}, f32[1,1024]{1,0:T(1,128)}, f32[48,1024]{1,0:T(8,128)}) custom-call(f32[2,4,6]{2,1,0:T(4,128)} %cam.3, f32[3,1024]{1,0:T(4,128)} %pos.3, f32[3,1024]{1,0:T(4,128)} %scl.3, f32[4,1024]{1,0:T(4,128)} %rot.3, f32[1,1024]{1,0:T(1,128)} %bitcast.11, f32[48,1024]{1,0:T(8,128)} %col.3, ...), custom_call_target="tpu_custom_call" | custom-call | tf_op jit(solution)/shard_map/pallas_call | solution.py:764

commit v4 on v3

--- a/solution.py
+++ b/solution.py
@@ -312,6 +312,17 @@
     place_ref,
     count_ref,
     cam,
+    far_pos,
+    far_scl,
+    far_rot,
+    far_opa,
+    far_col,
+    far_fetch,
+    far_lists,
+    far_target,
+    table,
+    back,
+    back_o,
     pos,
     scl,
     rot,
@@ -320,9 +331,6 @@
     fetch,
     lists,
     target,
-    table,
-    back,
-    back_o,
     mine,
     flat,
     wide,
@@ -368,15 +376,23 @@
     own_h,
     own_i,
     own_j,
+    loads,
 ):
     c, t = place()
     me = c * N_TILE + t
+    fars = (far_pos, far_scl, far_rot, far_opa, far_col, far_fetch, far_lists, far_target)
+    nears = (pos, scl, rot, opa, col, fetch, lists, target)
+    copies = [pltpu.make_async_copy(far, near, loads.at[k]) for k, (far, near) in enumerate(zip(fars, nears))]
+    for copy in copies:
+        copy.start()
     barrier = greet(c, t)
+    for k, value in enumerate(view_of(cam, lax.broadcasted_iota(jnp.int32, (8, 128), 1) // 16)):
+        view_ref[k] = value
+    for copy in copies:
+        copy.wait()
     block = [fetch[p, 0, 0:1, 0:1] // 16 for p in range(2)]
     half = lax.broadcasted_iota(jnp.int32, (1, 128), 1) < 64
     mine[0, :, :] = jnp.where(half, jnp.broadcast_to(block[0], (1, 128)), jnp.broadcast_to(block[1], (1, 128)))
-    for k, value in enumerate(view_of(cam, lax.broadcasted_iota(jnp.int32, (8, 128), 1) // 16)):
-        view_ref[k] = value
     expand((pos, scl, rot, opa, col), flat, wide)
 
     def step(chunk, carry):
@@ -723,9 +739,13 @@
             shape(N_DEV, 2, 128),
             shape(N_CAM, 64, 128),
         ),
-        in_specs=[SMEM] * 3 + [VMEM] * 8,
+        in_specs=[SMEM] * 3 + [pl.BlockSpec(memory_space=pl.ANY)] * 8,
         out_specs=(VMEM,) * 3,
         scratch_shapes=[
+            *[pltpu.VMEM((n, 1024), F32) for n in (3, 3, 4, 1, 48)],
+            pltpu.VMEM((2, N_CAM, 8, N_TILE), jnp.int32),
+            pltpu.VMEM((2, 1, LIST), jnp.int32),
+            pltpu.VMEM((2, 3, 1, PIX), F32),
             pltpu.VMEM((1, 1, 128), jnp.int32),
             pltpu.VMEM((64, 1024), F32),
             pltpu.VMEM((512, 8, 128), F32),
@@ -749,7 +769,8 @@
             pltpu.VMEM((2, LIST, 128), F32),
             pltpu.VMEM((LIST, 2 * 128), F32),
         ]
-        + [DMA] * 23,
+        + [DMA] * 23
+        + [DMA((8,))],
         compiler_params=pltpu.CompilerParams(collective_id=0, has_side_effects=True),
     )(
         tile_ids.reshape(2),

time: 55.4 us -> 55.3 us (level)
  no operation moved by 1% of the time
where the time goes in v4:
time: 55.3 us; the launch traced here: 55.1 us
  Pallas kernels  54.5 us (99%)
  between operations  0.64 us (1%)
    pallas_call x1, Pallas kernels, body(): pl.pallas_call(main_kernel, out_shape=(shape(N_DEV, 1, 128, dtype=jnp.int...  50.1 us
    pallas_call x1, Pallas kernels, body(): pl.pallas_call(gradient_kernel, out_shape=tuple((shape(n, 1024) for n in...  4.35 us

profile of v4, /device:TPU:1, one launch (start us, length us, event | category | flops | bytes accessed | tf_op | source)
XLA Modules:
  0.0 55.1 jit_solution(11372396321162495602)
XLA Ops:
  0.6 50.1 %shard_map.146 = (s32[256,1,128]{2,1,0:T(1,128)}, f32[256,2,128]{2,1,0:T(2,128)}, f32[4,64,128]{2,1,0:T(8,128)}) custom-call(s32[2]{0:T(128)} %bitcast.14, s32[2]{0:T(128)} %bitcast.15, f32[2,4,6]{2,1,0:T(4,128)} %cam.3, f32[3,1024]{1,0:T(4,128)} %pos.1, f32[3,1024]{1,0:T(4,128)} %scl.1, f32[4,1024]{1,0:T(4,128)} %rot.1, f32[1,1024]{1,0:T(1,128)} %bitcast.10, ...), custom_call_target="tpu_custom_call" | custom-call | tf_op jit(solution)/shard_map/pallas_call | solution.py:735
  50.8 4.4 %shard_map.147 = (f32[3,1024]{1,0:T(4,128)}, f32[3,1024]{1,0:T(4,128)}, f32[4,1024]{1,0:T(4,128)}, f32[1,1024]{1,0:T(1,128)}, f32[48,1024]{1,0:T(8,128)}) custom-call(f32[2,4,6]{2,1,0:T(4,128)} %cam.3, f32[3,1024]{1,0:T(4,128)} %pos.1, f32[3,1024]{1,0:T(4,128)} %scl.1, f32[4,1024]{1,0:T(4,128)} %rot.1, f32[1,1024]{1,0:T(1,128)} %bitcast.11, f32[48,1024]{1,0:T(8,128)} %col.1, ...), custom_call_target="tpu_custom_call" | custom-call | tf_op jit(solution)/shard_map/pallas_call | solution.py:785
